TPU v7x, 32 devices: a whole 2x2x4 slice. The times are simulated.
32 devices in a mesh: dp: 8 (over z, x), tensor: 4 (over y, core).
Axes of the slice: x: 2, y: 2, z: 4, core: 2. Of those that a mesh axis runs over, the one named last changes fastest.
Arguments:
- tokens: bfloat16 [4096, 768], P(('dp', 'tensor')), may hold values from -20 to 20
- condition: bfloat16 [16, 768], P('dp'), may hold values from -4 to 4
- adaptive_weight: bfloat16 [768, 6, 768], P('dp', None, 'tensor'), may hold values from -0.21875 to 0.21875
- adaptive_bias: float32 [6, 768], P(None, 'tensor'), may hold values from -3 to 3
- entry_weight: bfloat16 [768, 3, 768], P('dp', None, 'tensor'), may hold values from -1 to 1
- entry_bias: float32 [2, 768], P(None, 'tensor'), may hold values from -3 to 3
- output_weight: bfloat16 [768, 768], P('tensor', 'dp'), may hold values from -0.875 to 0.875
- output_bias: float32 [768], replicated, may hold values from -3 to 3
- expand_weight: bfloat16 [768, 3072], P('dp', 'tensor'), may hold values from -0.21875 to 0.21875
- expand_bias: float32 [3072], P('tensor'), may hold values from -3 to 3
- reduce_weight: bfloat16 [3072, 768], P('tensor', 'dp'), may hold values from -0.109375 to 0.109375
- reduce_bias: float32 [768], replicated, may hold values from -3 to 3
- cotangent: bfloat16 [4096, 768], P(('dp', 'tensor')), may hold values from -6 to 6
Outputs:
- block_output: bfloat16 [4096, 768], P(('dp', 'tensor'))
- tokens_gradient: float32 [4096, 768], P(('dp', 'tensor'))
- condition_gradient: float32 [16, 768], P('dp')
- adaptive_gradient: float32 [768, 6, 768], P('dp', None, 'tensor')
- bias_adaptive: float32 [6, 768], P(None, 'tensor')
- entry_gradient: float32 [768, 3, 768], P('dp', None, 'tensor')
- bias_entry: float32 [2, 768], P(None, 'tensor')
- output_gradient: float32 [768, 768], P('tensor', 'dp')
- bias_output: float32 [768], replicated
- expand_gradient: float32 [768, 3072], P('dp', 'tensor')
- bias_expand: float32 [3072], P('tensor')
- reduce_gradient: float32 [3072, 768], P('tensor', 'dp')
- bias_reduce: float32 [768], replicated
All inputs are finite; a program needn't handle non-finite values.
Results may differ from a plain program's by a relative error of at most 0.015.
The roundings to bfloat16 on the way count: a program that leaves them out, or rounds other values in their place, can miss the bound.
Values may be sent and summed in bfloat16 or wider, within the bound.
A program may use at most 128 MiB of HBM per device.

v0:
```python
import jax
import jax.numpy as jnp
from jax import lax
from jax.sharding import PartitionSpec as P

HEAD_DIM = 64
LEN = 256


NORM_EPSILON = 1e-06
GELU_ROOT = 0.7978845608028654
GELU_CUBIC = 0.044715
HIGHEST_PRECISION = lax.Precision.HIGHEST


def norm_rows(values):
    center = values - jnp.mean(values, axis=-1, keepdims=True)
    inverse = lax.rsqrt(jnp.mean(center * center, axis=-1, keepdims=True) + NORM_EPSILON)
    return (center * inverse, inverse)


def norm_back(upstream, normed, inverse):
    return inverse * (
        upstream
        - jnp.mean(upstream, axis=-1, keepdims=True)
        - normed * jnp.mean(upstream * normed, axis=-1, keepdims=True)
    )


def gelu_pair(inputs):
    tangent = jnp.tanh(GELU_ROOT * (inputs + GELU_CUBIC * inputs * inputs * inputs))
    output = 0.5 * inputs * (1.0 + tangent)
    slope_value = 0.5 * (1.0 + tangent) + 0.5 * inputs * (1.0 - tangent * tangent) * GELU_ROOT * (
        1.0 + 3.0 * GELU_CUBIC * inputs * inputs
    )
    return (output, slope_value)


def contract_first(left, right):
    return lax.dot_general(
        left, right, (((0,), (0,)), ((), ())), preferred_element_type=jnp.float32
    )


def contract_last(left, right):
    return lax.dot_general(
        left, right, (((1,), (1,)), ((), ())), preferred_element_type=jnp.float32
    )


def gather_rows(values):
    return lax.all_gather(values, "tensor", axis=0, tiled=True)


def sum_rows(values):
    return lax.psum_scatter(
        values.astype(jnp.bfloat16), "tensor", scatter_dimension=0, tiled=True
    ).astype(jnp.float32)


def attend(query_rows, key_rows, value_rows):
    factor = query_rows.shape[-1] ** (-0.5)
    scores = (
        jnp.einsum("blhe,bmhe->bhlm", query_rows, key_rows, preferred_element_type=jnp.float32)
        * factor
    )
    row_top = jnp.max(scores, axis=-1, keepdims=True)
    log_total = row_top + jnp.log(jnp.sum(jnp.exp(scores - row_top), axis=-1, keepdims=True))
    weights = jnp.exp(scores - log_total).astype(jnp.bfloat16)
    attended = jnp.einsum(
        "bhlm,bmhe->blhe", weights, value_rows, preferred_element_type=jnp.float32
    )
    return (attended.astype(jnp.bfloat16), log_total)


def attend_back(query_rows, key_rows, value_rows, log_total, attended_grad):
    factor = query_rows.shape[-1] ** (-0.5)
    scores = (
        jnp.einsum("blhe,bmhe->bhlm", query_rows, key_rows, preferred_element_type=jnp.float32)
        * factor
    )
    probability = jnp.exp(scores - log_total)
    weights = probability.astype(jnp.bfloat16)
    value_grad = jnp.einsum(
        "bhlm,blhe->bmhe", weights, attended_grad, preferred_element_type=jnp.float32
    )
    weight_grad = jnp.einsum(
        "blhe,bmhe->bhlm", attended_grad, value_rows, preferred_element_type=jnp.float32
    )
    row_inner = jnp.sum(probability * weight_grad, axis=-1, keepdims=True)
    score_grad = (probability * (weight_grad - row_inner) * factor).astype(jnp.bfloat16)
    query_grad = jnp.einsum(
        "bhlm,bmhe->blhe", score_grad, key_rows, preferred_element_type=jnp.float32
    )
    key_grad = jnp.einsum(
        "bhlm,blhe->bmhe", score_grad, query_rows, preferred_element_type=jnp.float32
    )
    return (query_grad, key_grad, value_grad)


def body(
    tokens,
    condition,
    adaptive_weight,
    adaptive_bias,
    entry_weight,
    entry_bias,
    output_weight,
    output_bias,
    expand_weight,
    expand_bias,
    reduce_weight,
    reduce_bias,
    cotangent,
):
    tensor_index = lax.axis_index("tensor")
    tensor_count = lax.axis_size("tensor")
    row_count = tokens.shape[0]
    features = tokens.shape[1]
    seq_count = condition.shape[0]
    local_width = adaptive_bias.shape[1]
    local_hidden = expand_bias.shape[0]
    group_rows = row_count * tensor_count
    head_count = local_width // HEAD_DIM
    head_shape = (seq_count, LEN, head_count, HEAD_DIM)
    adaptive_full, entry_full, output_full, expand_full, reduce_full = (
        lax.all_gather(adaptive_weight, "dp", axis=0, tiled=True),
        lax.all_gather(entry_weight, "dp", axis=0, tiled=True),
        lax.all_gather(output_weight, "dp", axis=1, tiled=True),
        lax.all_gather(expand_weight, "dp", axis=0, tiled=True),
        lax.all_gather(reduce_weight, "dp", axis=1, tiled=True),
    )
    condition_float = condition.astype(jnp.float32)
    soft_condition = jax.nn.silu(condition_float).astype(jnp.bfloat16)
    modulation_local = (
        jnp.dot(
            soft_condition,
            adaptive_full.reshape(features, 6 * local_width),
            preferred_element_type=jnp.float32,
        ).reshape(seq_count, 6, local_width)
        + adaptive_bias[None]
    )
    modulation = lax.all_gather(modulation_local, "tensor", axis=2, tiled=True)
    seq_of_row = (tensor_index * row_count + jnp.arange(row_count, dtype=jnp.int32)) // LEN
    selector = (seq_of_row[:, None] == jnp.arange(seq_count, dtype=jnp.int32)[None, :]).astype(
        jnp.float32
    )
    per_row = jnp.dot(
        selector, modulation.reshape(seq_count, 6 * features), precision=HIGHEST_PRECISION
    ).reshape(row_count, 6, features)
    shift_one, scale_one, gate_one, shift_two, scale_two, gate_two = [
        per_row[:, column] for column in range(6)
    ]
    inputs = tokens.astype(jnp.float32)
    normed_one, inverse_one = norm_rows(inputs)
    attention_local = (normed_one * (1.0 + scale_one) + shift_one).astype(jnp.bfloat16)
    attention_input = gather_rows(attention_local)
    projected = jnp.dot(
        attention_input,
        entry_full.reshape(features, 3 * local_width),
        preferred_element_type=jnp.float32,
    ).reshape(group_rows, 3, local_width)
    query_rows = (projected[:, 0] + entry_bias[0]).astype(jnp.bfloat16).reshape(head_shape)
    key_rows = projected[:, 1].astype(jnp.bfloat16).reshape(head_shape)
    value_rows = (projected[:, 2] + entry_bias[1]).astype(jnp.bfloat16).reshape(head_shape)
    attended, log_total = attend(query_rows, key_rows, value_rows)
    attended = attended.reshape(group_rows, local_width)
    attention_branch = (
        sum_rows(jnp.dot(attended, output_full, preferred_element_type=jnp.float32)) + output_bias
    )
    middle = inputs + gate_one * attention_branch
    normed_two, inverse_two = norm_rows(middle)
    feed_local = (normed_two * (1.0 + scale_two) + shift_two).astype(jnp.bfloat16)
    feed_input = gather_rows(feed_local)
    hidden_pre = jnp.dot(feed_input, expand_full, preferred_element_type=jnp.float32) + expand_bias
    hidden_value, hidden_slope = gelu_pair(hidden_pre)
    hidden_rows = hidden_value.astype(jnp.bfloat16)
    feed_branch = (
        sum_rows(jnp.dot(hidden_rows, reduce_full, preferred_element_type=jnp.float32))
        + reduce_bias
    )
    block_output = (middle + gate_two * feed_branch).astype(jnp.bfloat16)
    adaptive_back, entry_back, output_back, expand_back, reduce_back = (
        lax.all_gather(adaptive_weight, "dp", axis=0, tiled=True),
        lax.all_gather(entry_weight, "dp", axis=0, tiled=True),
        lax.all_gather(output_weight, "dp", axis=1, tiled=True),
        lax.all_gather(expand_weight, "dp", axis=0, tiled=True),
        lax.all_gather(reduce_weight, "dp", axis=1, tiled=True),
    )
    upstream = cotangent.astype(jnp.float32)
    feed_grad = upstream * gate_two
    feed_gathered = gather_rows(feed_grad.astype(jnp.bfloat16))
    reduce_total = contract_first(hidden_rows, feed_gathered)
    hidden_grad = contract_last(feed_gathered, reduce_back) * hidden_slope
    hidden_round = hidden_grad.astype(jnp.bfloat16)
    expand_total = contract_first(feed_input, hidden_round)
    feed_input_grad = sum_rows(contract_last(hidden_round, expand_back))
    middle_grad = upstream + norm_back(feed_input_grad * (1.0 + scale_two), normed_two, inverse_two)
    attention_grad = middle_grad * gate_one
    attention_gathered = gather_rows(attention_grad.astype(jnp.bfloat16))
    output_total = contract_first(attended, attention_gathered)
    attended_grad = (
        contract_last(attention_gathered, output_back).astype(jnp.bfloat16).reshape(head_shape)
    )
    query_grad, key_grad, value_grad = attend_back(
        query_rows, key_rows, value_rows, log_total, attended_grad
    )
    query_grad = query_grad.reshape(group_rows, local_width)
    key_grad = key_grad.reshape(group_rows, local_width)
    value_grad = value_grad.reshape(group_rows, local_width)
    entry_round = (
        jnp.stack([query_grad, key_grad, value_grad], axis=1)
        .astype(jnp.bfloat16)
        .reshape(group_rows, 3 * local_width)
    )
    entry_total = contract_first(attention_input, entry_round).reshape(features, 3, local_width)
    input_grad = sum_rows(contract_last(entry_round, entry_back.reshape(features, 3 * local_width)))
    tokens_gradient = middle_grad + norm_back(
        input_grad * (1.0 + scale_one), normed_one, inverse_one
    )
    row_terms = jnp.stack(
        [
            input_grad,
            input_grad * normed_one,
            middle_grad * attention_branch,
            feed_input_grad,
            feed_input_grad * normed_two,
            upstream * feed_branch,
        ],
        axis=1,
    )
    per_sequence = lax.dot_general(
        selector,
        row_terms.reshape(row_count, 6 * features),
        (((0,), (0,)), ((), ())),
        precision=HIGHEST_PRECISION,
        preferred_element_type=jnp.float32,
    ).reshape(seq_count, 6, features)
    modulation_grad = lax.psum_scatter(
        per_sequence.astype(jnp.bfloat16), "tensor", scatter_dimension=2, tiled=True
    ).astype(jnp.float32)
    modulation_round = modulation_grad.astype(jnp.bfloat16).reshape(seq_count, 6 * local_width)
    adaptive_total = contract_first(soft_condition, modulation_round).reshape(
        features, 6, local_width
    )
    condition_partial = contract_last(
        modulation_round, adaptive_back.reshape(features, 6 * local_width)
    )
    condition_sum = lax.psum(condition_partial, "tensor")
    sigmoid_value = jax.nn.sigmoid(condition_float)
    condition_gradient = (
        condition_sum * sigmoid_value * (1.0 + condition_float * (1.0 - sigmoid_value))
    )
    adaptive_gradient, entry_gradient, output_gradient, expand_gradient, reduce_gradient = (
        lax.psum_scatter(adaptive_total, "dp", scatter_dimension=0, tiled=True),
        lax.psum_scatter(entry_total, "dp", scatter_dimension=0, tiled=True),
        lax.psum_scatter(output_total, "dp", scatter_dimension=1, tiled=True),
        lax.psum_scatter(expand_total, "dp", scatter_dimension=0, tiled=True),
        lax.psum_scatter(reduce_total, "dp", scatter_dimension=1, tiled=True),
    )
    width_start = tensor_index * local_width
    hidden_start = tensor_index * local_hidden
    adaptive_slot = lax.dynamic_update_slice_in_dim(
        jnp.zeros((6, features), jnp.float32), jnp.sum(modulation_grad, axis=0), width_start, 1
    )
    entry_slot = lax.dynamic_update_slice_in_dim(
        jnp.zeros((2, features), jnp.float32),
        jnp.stack([jnp.sum(query_grad, axis=0), jnp.sum(value_grad, axis=0)]),
        width_start,
        1,
    )
    expand_slot = lax.dynamic_update_slice_in_dim(
        jnp.zeros((local_hidden * tensor_count,), jnp.float32),
        jnp.sum(hidden_grad, axis=0),
        hidden_start,
        0,
    )
    adaptive_sums, entry_sums, output_sums, expand_sums, reduce_sums = lax.psum(
        (
            adaptive_slot,
            entry_slot,
            jnp.sum(attention_grad, axis=0),
            expand_slot,
            jnp.sum(feed_grad, axis=0),
        ),
        ("dp", "tensor"),
    )
    bias_adaptive = lax.dynamic_slice_in_dim(adaptive_sums, width_start, local_width, 1)
    bias_entry = lax.dynamic_slice_in_dim(entry_sums, width_start, local_width, 1)
    bias_expand = lax.dynamic_slice_in_dim(expand_sums, hidden_start, local_hidden, 0)
    return (
        block_output,
        tokens_gradient,
        condition_gradient,
        adaptive_gradient,
        bias_adaptive,
        entry_gradient,
        bias_entry,
        output_gradient,
        output_sums,
        expand_gradient,
        bias_expand,
        reduce_gradient,
        reduce_sums,
    )


def solution(mesh):
    in_specs = (
        P(("dp", "tensor"), None),
        P("dp", None),
        P("dp", None, "tensor"),
        P(None, "tensor"),
        P("dp", None, "tensor"),
        P(None, "tensor"),
        P("tensor", "dp"),
        P(),
        P("dp", "tensor"),
        P("tensor"),
        P("tensor", "dp"),
        P(),
        P(("dp", "tensor"), None),
    )
    out_specs = (
        P(("dp", "tensor"), None),
        P(("dp", "tensor"), None),
        P("dp", None),
        P("dp", None, "tensor"),
        P(None, "tensor"),
        P("dp", None, "tensor"),
        P(None, "tensor"),
        P("tensor", "dp"),
        P(),
        P("dp", "tensor"),
        P("tensor"),
        P("tensor", "dp"),
        P(),
    )
    return jax.shard_map(body, mesh=mesh, in_specs=in_specs, out_specs=out_specs, check_vma=False)
```

profile of v0, /device:TPU:0, one launch (start us, length us, event | category | flops | bytes accessed | tf_op | source)
XLA Modules:
  0.0 773.9 jit_solution(14435792287438220595)
XLA Ops:
  8.0 39.2 %all_gather.38 = bf16[768,3,192]{2,0,1:T(8,128)(2,1)S(1)} all-gather(bf16[96,3,192]{2,0,1:T(8,128)(2,1)} %param.17), channel_id=1, replica_groups=mesh['dp'=8,'tensor'=4] {'dp'}, dimensions={0}, use_global_device_ids=true | all-gather | bytes 995328 | tf_op jit(solution)/shard_map/all_gather | solution.py:128
  48.5 34.3 %all_gather.39 = bf16[192,768]{0,1:T(8,128)(2,1)} all-gather(bf16[192,96]{0,1:T(8,128)(2,1)S(1)} %copy.88), channel_id=1, replica_groups=mesh['dp'=8,'tensor'=4] {'dp'}, dimensions={1}, use_global_device_ids=true | all-gather | bytes 331776 | tf_op jit(solution)/shard_map/all_gather | solution.py:129
  82.9 2.8 copy.79
  86.4 8.9 %all_gather.36 = f32[2,6,768]{1,0,2:T(2,128)S(1)} all-gather(f32[2,6,192]{1,0,2:T(2,128)S(1)} %copy.80), channel_id=1, replica_groups=mesh['dp'=8,'tensor'=4] {'tensor'}, dimensions={2}, use_global_device_ids=true | all-gather | bytes 46080 | tf_op jit(solution)/shard_map/all_gather | solution.py:143
  97.1 8.7 %all_gather.37 = bf16[512,768]{1,0:T(8,128)(2,1)S(1)} all-gather(bf16[128,768]{1,0:T(8,128)(2,1)S(1)} %fusion.52), channel_id=1, replica_groups=mesh['dp'=8,'tensor'=4] {'tensor'}, dimensions={0}, use_global_device_ids=true | all-gather | bytes 983040 | tf_op jit(solution)/shard_map/all_gather | solution.py:52
  112.6 1.9 fusion.26
  118.2 20.9 %reduce-scatter.15.cloned.1.call-done = bf16[128,768]{1,0:T(8,128)(2,1)} async-done(((bf16[512,768]{1,0:T(8,128)(2,1)}), bf16[128,768]{1,0:T(8,128)(2,1)}) %reduce-scatter.15.cloned.1.call-update) | async-done | bytes 196624 | tf_op jit(solution)/shard_map/reduce_scatter | solution.py:56
  140.6 8.5 %all_gather.40 = bf16[512,768]{1,0:T(8,128)(2,1)} all-gather(bf16[128,768]{1,0:T(8,128)(2,1)S(1)} %get-tuple-element.34), channel_id=1, replica_groups=mesh['dp'=8,'tensor'=4] {'tensor'}, dimensions={0}, use_global_device_ids=true | all-gather | bytes 983040 | tf_op jit(solution)/shard_map/all_gather | solution.py:52
  149.0 9.1 %all_gather.43 = bf16[512,768]{1,0:T(8,128)(2,1)} all-gather(bf16[128,768]{1,0:T(8,128)(2,1)S(1)} %get-tuple-element.33), channel_id=1, replica_groups=mesh['dp'=8,'tensor'=4] {'tensor'}, dimensions={0}, use_global_device_ids=true | all-gather | bytes 983040 | tf_op jit(solution)/shard_map/all_gather | solution.py:52
  158.2 24.2 %all-gather.6.cloned.1.call-done = bf16[768,768]{1,0:T(8,128)(2,1)} async-done(((bf16[96,768]{1,0:T(8,128)(2,1)}), bf16[768,768]{1,0:T(8,128)(2,1)}) %all-gather.6.cloned.1.call-update) | async-done | bytes 1179664 | tf_op jit(solution)/shard_map/all_gather | solution.py:130
  182.4 3.5 convolution_add_fusion
  185.9 38.4 %all-gather.8.cloned.1.call-done = bf16[768,768]{0,1:T(8,128)(2,1)} async-done(((bf16[768,96]{0,1:T(8,128)(2,1)}), bf16[768,768]{0,1:T(8,128)(2,1)}) %all-gather.8.cloned.1.call-update) | async-done | bytes 1179664 | tf_op jit(solution)/shard_map/all_gather | solution.py:131
  224.3 4.1 fusion.123
  231.1 3.8 convolution_convert_fusion.1
  234.9 18.2 %reduce-scatter.19.cloned.1.call-done = bf16[128,768]{1,0:T(8,128)(2,1)} async-done(((bf16[512,768]{1,0:T(8,128)(2,1)}), bf16[128,768]{1,0:T(8,128)(2,1)}) %reduce-scatter.19.cloned.1.call-update) | async-done | bytes 196624 | tf_op jit(solution)/shard_map/reduce_scatter | solution.py:56
  254.7 24.0 %reduce-scatter.17.cloned.1.call-done = bf16[128,768]{1,0:T(8,128)(2,1)} async-done(((bf16[512,768]{1,0:T(8,128)(2,1)}), bf16[128,768]{1,0:T(8,128)(2,1)}) %reduce-scatter.17.cloned.1.call-update) | async-done | bytes 196624 | tf_op jit(solution)/shard_map/reduce_scatter | solution.py:56
  278.7 2.0 fusion.86
  280.7 8.2 %all_gather.44 = bf16[512,768]{1,0:T(8,128)(2,1)S(1)} all-gather(bf16[128,768]{1,0:T(8,128)(2,1)S(1)} %get-tuple-element.28), channel_id=1, replica_groups=mesh['dp'=8,'tensor'=4] {'tensor'}, dimensions={0}, use_global_device_ids=true | all-gather | bytes 983040 | tf_op jit(solution)/shard_map/all_gather | solution.py:52
  291.8 2.6 fusion.81
  294.5 4.9 fusion.120
  299.4 4.4 fusion.23
  303.9 3.1 fusion.119
  307.8 1.7 stack_reshape.9
  309.6 1.8 copy.94
  311.4 1.7 stack_reshape.10
  315.1 3.3 bitcast_convert_fusion
  318.5 23.8 %reduce-scatter.21.cloned.1.call-done = bf16[128,768]{1,0:T(8,128)(2,1)} async-done(((bf16[512,768]{1,0:T(8,128)(2,1)}), bf16[128,768]{1,0:T(8,128)(2,1)}) %reduce-scatter.21.cloned.1.call-update) | async-done | bytes 196624 | tf_op jit(solution)/shard_map/reduce_scatter | solution.py:56
  342.3 1.7 fusion.63
  344.0 1.9 fusion.65
  345.9 1.7 bitcast_dynamic-update-slice_fusion
  350.9 3.1 copy.98
  353.9 3.4 fusion.27
  357.3 2.7 copy.108
  360.0 2.7 reshape.177
  364.3 3.6 fusion.72
  369.1 3.8 fusion.115
  374.1 3.4 fusion.36
  377.7 5.0 reduce-scatter.31.cloned.1.call-done
  384.2 3.0 fusion.99
  394.1 55.1 %reduce-scatter.33.cloned.1.call-done = f32[96,192]{1,0:T(8,128)} async-done(((f32[768,192]{1,0:T(8,128)}), f32[96,192]{1,0:T(8,128)}) %reduce-scatter.33.cloned.1.call-update) | async-done | bytes 73744
  450.8 1.7 fusion.76
  454.8 42.1 %all-reduce = (f32[6,768]{1,0:T(8,128)S(1)}, f32[2,768]{1,0:T(2,128)S(1)}, f32[768]{0:T(1024)}, f32[3072]{0:T(1024)S(1)}, f32[768]{0:T(1024)}) all-reduce(f32[6,768]{1,0:T(8,128)S(1)} %dynamic_update_slice.9, f32[2,768]{1,0:T(2,128)} %dynamic_update_slice.10, ...), channel_id=1, replica_groups=mesh['dp'=8,'tensor'=4] {'dp','tensor'}, use_global_device_ids=true, to_apply=%region_19.20 | all-reduce | flops 10752 | bytes 86016 | tf_op jit(solution)/shard_map/psum | solution.py:278
  497.6 2.4 convolution_bitcast_fusion.2
  499.9 5.9 psum.42
  507.7 14.8 %reduce-scatter.27.cloned.1.call-done = f32[96,768]{1,0:T(8,128)} async-done(((f32[768,768]{1,0:T(8,128)}), f32[96,768]{1,0:T(8,128)}) %reduce-scatter.27.cloned.1.call-update) | async-done | bytes 294928 | tf_op jit(solution)/shard_map/reduce_scatter | solution.py:258
  522.6 72.9 %reduce-scatter.29.cloned.1.call-done = f32[768,96]{0,1:T(8,128)} async-done(((f32[768,768]{0,1:T(8,128)}), f32[768,96]{0,1:T(8,128)}) %reduce-scatter.29.cloned.1.call-update) | async-done | bytes 294928 | tf_op jit(solution)/shard_map/reduce_scatter | solution.py:259
  595.5 72.7 %reduce-scatter.25.cloned.1.call-done = f32[96,3,192]{2,0,1:T(8,128)} async-done(((f32[768,3,192]{2,0,1:T(8,128)}), f32[96,3,192]{2,0,1:T(8,128)}) %reduce-scatter.25.cloned.1.call-update) | async-done | bytes 221200 | tf_op jit(solution)/shard_map/reduce_scatter | solution.py:256
  668.2 99.1 %reduce-scatter.23.cloned.1.call-done = f32[96,6,192]{2,0,1:T(8,128)} async-done(((f32[768,6,192]{2,0,1:T(8,128)}), f32[96,6,192]{2,0,1:T(8,128)}) %reduce-scatter.23.cloned.1.call-update) | async-done | bytes 442384 | tf_op jit(solution)/shard_map/reduce_scatter | solution.py:255
  (186 shorter events, 48.6 us)
Async XLA Ops:
  7.2 75.7 %all-gather.4.cloned.1.call-start = ((), (), s32[]{:S(2)}) async-start(), calls=%async_computation.10 | async-start | bytes 2654208 | tf_op jit(solution)/shard_map/all_gather | solution.py:127
  7.9 131.2 %reduce-scatter.15.cloned.1.call-start = ((), (), s32[]{:S(2)}) async-start(), calls=%async_computation.11 | async-start | bytes 983040 | tf_op jit(solution)/shard_map/reduce_scatter | solution.py:56
  8.0 39.9 %copy-start.42 = (f32[2,192]{1,0:T(2,128)S(1)}, f32[2,192]{1,0:T(2,128)}, u32[]{:S(2)}) copy-start(f32[2,192]{1,0:T(2,128)} %param.18) | copy-start | bytes 4612
  8.0 40.1 %copy-start.27 = (bf16[192,96]{1,0:T(8,128)(2,1)S(1)}, bf16[192,96]{1,0:T(8,128)(2,1)}, u32[]{:S(2)}) copy-start(bf16[192,96]{1,0:T(8,128)(2,1)} %param.19) | copy-start | bytes 110596
  8.0 40.2 %copy-start.1 = (bf16[128,768]{1,0:T(8,128)(2,1)S(1)}, bf16[128,768]{1,0:T(8,128)(2,1)}, u32[]{:S(2)}) copy-start(bf16[128,768]{1,0:T(8,128)(2,1)} %param.13) | copy-start | bytes 589828
  47.2 35.6 %copy-start.6 = (bf16[768,3,192]{2,0,1:T(8,128)(2,1)}, bf16[768,3,192]{2,0,1:T(8,128)(2,1)S(1)}, u32[]{:S(2)}) copy-start(bf16[768,3,192]{2,0,1:T(8,128)(2,1)S(1)} %all_gather.38) | copy-start | bytes 2654212
  48.0 62.4 %copy-start.38 = (f32[3,64]{1,0:T(4,128)}, f32[3,64]{1,0:T(4,128)S(1)}, u32[]{:S(2)}) copy-start(f32[3,64]{1,0:T(4,128)S(1)} %add.200) | copy-start | bytes 2308
  48.2 47.6 %copy-start.43 = (s32[128]{0:T(128)}, s32[128]{0:T(128)S(1)}, u32[]{:S(2)}) copy-start(s32[128]{0:T(128)S(1)} %and_select_fusion) | copy-start | bytes 1540
  48.3 48.6 %copy-start.32 = (f32[128]{0:T(128)}, f32[128]{0:T(128)S(1)}, u32[]{:S(2)}) copy-start(f32[128]{0:T(128)S(1)} %broadcast_multiply_fusion.5) | copy-start | bytes 1540
  82.8 14.1 %copy-start.37 = (f32[128]{0:T(128)}, f32[128]{0:T(128)S(1)}, u32[]{:S(2)}) copy-start(f32[128]{0:T(128)S(1)} %add_rsqrt_fusion.1) | copy-start | bytes 1540
  109.2 3.0 copy-start.18
  112.5 4.3 copy-start.7
  112.6 2.9 copy-start.8
  114.5 24.6 %copy-start.29 = (f32[768]{0:T(1024)S(1)}, f32[768]{0:T(1024)}, u32[]{:S(2)}) copy-start(f32[768]{0:T(1024)} %param.20) | copy-start | bytes 9220
  116.8 23.5 %copy-start.14 = (bf16[128,768]{1,0:T(8,128)(2,1)S(1)}, bf16[128,768]{1,0:T(8,128)(2,1)}, u32[]{:S(2)}) copy-start(bf16[128,768]{1,0:T(8,128)(2,1)} %param.25) | copy-start | bytes 589828
  116.9 65.5 %all-gather.6.cloned.1.call-start = ((), (), s32[]{:S(2)}) async-start(), calls=%async_computation.12 | async-start | bytes 1327104 | tf_op jit(solution)/shard_map/all_gather | solution.py:130
  117.6 106.7 %all-gather.8.cloned.1.call-start = ((), (), s32[]{:S(2)}) async-start(), calls=%async_computation.13 | async-start | bytes 1327104 | tf_op jit(solution)/shard_map/all_gather | solution.py:131
  118.2 134.9 %reduce-scatter.19.cloned.1.call-start = ((), (), s32[]{:S(2)}) async-start(), calls=%async_computation.15 | async-start | bytes 983040 | tf_op jit(solution)/shard_map/reduce_scatter | solution.py:56
  140.2 8.9 %copy-start.34 = (f32[128]{0:T(128)}, f32[128]{0:T(128)S(1)}, u32[]{:S(2)}) copy-start(f32[128]{0:T(128)S(1)} %broadcast_multiply_fusion.4) | copy-start | bytes 1540
  140.4 8.7 %copy-start.40 = (f32[128]{0:T(128)}, f32[128]{0:T(128)S(1)}, u32[]{:S(2)}) copy-start(f32[128]{0:T(128)S(1)} %add_rsqrt_fusion) | copy-start | bytes 1540
  224.3 5.0 copy-start.45
  231.0 22.1 %copy-start.35 = (f32[128]{0:T(128)S(1)}, f32[128]{0:T(128)}, u32[]{:S(2)}) copy-start(f32[128]{0:T(128)} %copy-done.34) | copy-start | bytes 1540
  231.0 22.1 %copy-start.41 = (f32[128]{0:T(128)S(1)}, f32[128]{0:T(128)}, u32[]{:S(2)}) copy-start(f32[128]{0:T(128)} %copy-done.40) | copy-start | bytes 1540
  231.0 47.7 %reduce-scatter.17.cloned.1.call-start = ((), (), s32[]{:S(2)}) async-start(), calls=%async_computation.14 | async-start | bytes 983040 | tf_op jit(solution)/shard_map/reduce_scatter | solution.py:56
  234.9 107.4 %reduce-scatter.21.cloned.1.call-start = ((), (), s32[]{:S(2)}) async-start(), calls=%async_computation.16 | async-start | bytes 983040 | tf_op jit(solution)/shard_map/reduce_scatter | solution.py:56
  278.7 11.1 %copy-start.9 = (bf16[192,768]{0,1:T(8,128)(2,1)S(1)}, bf16[192,768]{0,1:T(8,128)(2,1)}, u32[]{:S(2)}) copy-start(bf16[192,768]{0,1:T(8,128)(2,1)} %all_gather.39) | copy-start | bytes 884740
  280.7 65.3 %copy-start.4 = (f32[128,768]{1,0:T(8,128)}, f32[128,768]{1,0:T(8,128)S(1)}, u32[]{:S(2)}) copy-start(f32[128,768]{1,0:T(8,128)S(1)} %get-tuple-element.29) | copy-start | bytes 1179652
  294.5 5.0 copy-start.39
  303.9 3.1 copy-start.26
  306.9 6.2 copy-start.20
  315.0 3.4 copy-start.25
  315.1 29.0 %copy-start.33 = (f32[128]{0:T(128)S(1)}, f32[128]{0:T(128)}, u32[]{:S(2)}) copy-start(f32[128]{0:T(128)} %copy-done.32) | copy-start | bytes 1540
  318.4 27.5 %copy-start.30 = (f32[768]{0:T(1024)S(1)}, f32[768]{0:T(1024)}, u32[]{:S(2)}) copy-start(f32[768]{0:T(1024)} %param.20) | copy-start | bytes 9220
  318.4 29.3 %copy-start.13 = (bf16[128,768]{1,0:T(8,128)(2,1)S(1)}, bf16[128,768]{1,0:T(8,128)(2,1)}, u32[]{:S(2)}) copy-start(bf16[128,768]{1,0:T(8,128)(2,1)} %reduce-scatter.19.cloned.1.call-done) | copy-start | bytes 589828
  318.4 64.3 %reduce-scatter.31.cloned.1.call-start = ((), (), s32[]{:S(2)}) async-start(), calls=%async_computation.21 | async-start | bytes 245760
  344.0 6.0 copy-start.15
  344.0 6.0 copy-start.21
  344.0 6.0 copy-start.31
  350.9 3.1 copy-start.44
  357.3 5.5 copy-start.3
  357.3 5.5 copy-start.17
  362.8 86.4 %reduce-scatter.33.cloned.1.call-start = ((), (), s32[]{:S(2)}) async-start(), calls=%async_computation.22 | async-start | bytes 884736
  364.2 158.3 %reduce-scatter.27.cloned.1.call-start = ((), (), s32[]{:S(2)}) async-start(), calls=%async_computation.19 | async-start | bytes 2654208 | tf_op jit(solution)/shard_map/reduce_scatter | solution.py:258
  368.0 227.5 %reduce-scatter.29.cloned.1.call-start = ((), (), s32[]{:S(2)}) async-start(), calls=%async_computation.20 | async-start | bytes 2654208 | tf_op jit(solution)/shard_map/reduce_scatter | solution.py:259
  372.9 295.3 %reduce-scatter.25.cloned.1.call-start = ((), (), s32[]{:S(2)}) async-start(), calls=%async_computation.18 | async-start | bytes 2654208 | tf_op jit(solution)/shard_map/reduce_scatter | solution.py:256
  377.4 389.9 %reduce-scatter.23.cloned.1.call-start = ((), (), s32[]{:S(2)}) async-start(), calls=%async_computation.17 | async-start | bytes 5308416 | tf_op jit(solution)/shard_map/reduce_scatter | solution.py:255
  387.2 63.6 %copy-start.5 = (f32[128,768]{1,0:T(8,128)S(1)}, f32[128,768]{1,0:T(8,128)}, u32[]{:S(2)}) copy-start(f32[128,768]{1,0:T(8,128)} %copy-done.4) | copy-start | bytes 1179652
  387.2 63.6 %copy-start.10 = (bf16[128,768]{1,0:T(8,128)(2,1)S(1)}, bf16[128,768]{1,0:T(8,128)(2,1)}, u32[]{:S(2)}) copy-start(bf16[128,768]{1,0:T(8,128)(2,1)} %reduce-scatter.21.cloned.1.call-done) | copy-start | bytes 589828
  (11 other events, 16.2 us)
Sparse Core Ops, SparseCore 0:
  10.2 65.9 all-gather.3
  117.0 22.0 reduce-scatter.14
  141.3 41.0 all-gather.5
  184.4 39.8 all-gather.7
  231.1 21.9 reduce-scatter.18
  255.5 23.1 reduce-scatter.16
  318.5 23.7 reduce-scatter.20
  362.9 19.7 reduce-scatter.30
  386.0 63.1 reduce-scatter.32
  453.1 69.3 reduce-scatter.26
  526.6 68.8 reduce-scatter.28
  599.4 68.7 reduce-scatter.24
  672.4 94.8 reduce-scatter.22
where the time goes:
time: 775 us; the launch traced here: 774 us
  waiting for transfers between devices  471 us (61%)
  blocking collectives  165 us (21%)
  matrix products  59.7 us (8%)
  local copies, waits for them, and re-layouts  43.4 us (6%)
  other arithmetic  19.6 us (3%)
  between operations  14.4 us (2%)
    reduce_scatter x1, waiting for transfers between devices, body(): lax.psum_scatter(adaptive_total, 'dp', scatter_dimension=0, tiled=True)  99.1 us
    reduce_scatter x4, waiting for transfers between devices, sum_rows(): lax.psum_scatter(values.astype(jnp.bfloat16), 'tensor', scatter_dimension...  86.8 us
    reduce_scatter x1, waiting for transfers between devices, body(): lax.psum_scatter(reduce_total, 'dp', scatter_dimension=1, tiled=True)  72.9 us
    reduce_scatter x1, waiting for transfers between devices, body(): lax.psum_scatter(entry_total, 'dp', scatter_dimension=0, tiled=True)  72.7 us
    unnamed x15, waiting for transfers between devices  62.1 us
    psum x1, blocking collectives, body(): lax.psum((adaptive_slot, entry_slot, jnp.sum(attention_grad, axis=0), exp...  42.1 us
    all_gather x1, blocking collectives, body(): lax.all_gather(entry_weight, 'dp', axis=0, tiled=True)  39.2 us
    all_gather x1, waiting for transfers between devices, body(): lax.all_gather(reduce_weight, 'dp', axis=1, tiled=True)  38.4 us
  transfers between devices with their start and end apart: 13, of which 12 were waited for; matrix products, arithmetic and copies ran while one was open for 6% of the time, Pallas kernels for 0%

commit v1 on v0

--- a/solution.py
+++ b/solution.py
@@ -56,6 +56,19 @@
     return lax.psum_scatter(
         values.astype(jnp.bfloat16), "tensor", scatter_dimension=0, tiled=True
     ).astype(jnp.float32)
+
+
+def gather_weights(shards):
+    return [lax.all_gather(shard, "dp", axis=0, tiled=True) for shard in shards]
+
+
+def scatter_gradients(totals):
+    return [
+        lax.psum_scatter(
+            total.astype(jnp.bfloat16), "dp", scatter_dimension=0, tiled=True
+        ).astype(jnp.float32)
+        for total in totals
+    ]
 
 
 def attend(query_rows, key_rows, value_rows):
@@ -123,21 +136,23 @@
     group_rows = row_count * tensor_count
     head_count = local_width // HEAD_DIM
     head_shape = (seq_count, LEN, head_count, HEAD_DIM)
-    adaptive_full, entry_full, output_full, expand_full, reduce_full = (
-        lax.all_gather(adaptive_weight, "dp", axis=0, tiled=True),
-        lax.all_gather(entry_weight, "dp", axis=0, tiled=True),
-        lax.all_gather(output_weight, "dp", axis=1, tiled=True),
-        lax.all_gather(expand_weight, "dp", axis=0, tiled=True),
-        lax.all_gather(reduce_weight, "dp", axis=1, tiled=True),
+    dp_index = lax.axis_index("dp")
+    dp_count = lax.axis_size("dp")
+    shard_rows = adaptive_weight.shape[0]
+    entry_flat = entry_weight.reshape(shard_rows, 3 * local_width)
+    entry_full, output_full, expand_full, reduce_full = gather_weights(
+        (entry_flat, output_weight.T, expand_weight, reduce_weight.T)
     )
     condition_float = condition.astype(jnp.float32)
-    soft_condition = jax.nn.silu(condition_float).astype(jnp.bfloat16)
+    condition_all = lax.all_gather(condition, "dp", axis=0, tiled=True)
+    soft_all = jax.nn.silu(condition_all.astype(jnp.float32)).astype(jnp.bfloat16)
+    soft_mine = lax.dynamic_slice_in_dim(soft_all, dp_index * shard_rows, shard_rows, 1)
+    adaptive_flat = adaptive_weight.reshape(shard_rows, 6 * local_width)
+    modulation_partial = jnp.dot(soft_mine, adaptive_flat, preferred_element_type=jnp.float32)
     modulation_local = (
-        jnp.dot(
-            soft_condition,
-            adaptive_full.reshape(features, 6 * local_width),
-            preferred_element_type=jnp.float32,
-        ).reshape(seq_count, 6, local_width)
+        lax.psum_scatter(modulation_partial, "dp", scatter_dimension=0, tiled=True).reshape(
+            seq_count, 6, local_width
+        )
         + adaptive_bias[None]
     )
     modulation = lax.all_gather(modulation_local, "tensor", axis=2, tiled=True)
@@ -157,7 +172,7 @@
     attention_input = gather_rows(attention_local)
     projected = jnp.dot(
         attention_input,
-        entry_full.reshape(features, 3 * local_width),
+        entry_full,
         preferred_element_type=jnp.float32,
     ).reshape(group_rows, 3, local_width)
     query_rows = (projected[:, 0] + entry_bias[0]).astype(jnp.bfloat16).reshape(head_shape)
@@ -166,7 +181,7 @@
     attended, log_total = attend(query_rows, key_rows, value_rows)
     attended = attended.reshape(group_rows, local_width)
     attention_branch = (
-        sum_rows(jnp.dot(attended, output_full, preferred_element_type=jnp.float32)) + output_bias
+        sum_rows(contract_last(attended, output_full)) + output_bias
     )
     middle = inputs + gate_one * attention_branch
     normed_two, inverse_two = norm_rows(middle)
@@ -176,31 +191,26 @@
     hidden_value, hidden_slope = gelu_pair(hidden_pre)
     hidden_rows = hidden_value.astype(jnp.bfloat16)
     feed_branch = (
-        sum_rows(jnp.dot(hidden_rows, reduce_full, preferred_element_type=jnp.float32))
+        sum_rows(contract_last(hidden_rows, reduce_full))
         + reduce_bias
     )
     block_output = (middle + gate_two * feed_branch).astype(jnp.bfloat16)
-    adaptive_back, entry_back, output_back, expand_back, reduce_back = (
-        lax.all_gather(adaptive_weight, "dp", axis=0, tiled=True),
-        lax.all_gather(entry_weight, "dp", axis=0, tiled=True),
-        lax.all_gather(output_weight, "dp", axis=1, tiled=True),
-        lax.all_gather(expand_weight, "dp", axis=0, tiled=True),
-        lax.all_gather(reduce_weight, "dp", axis=1, tiled=True),
-    )
     upstream = cotangent.astype(jnp.float32)
     feed_grad = upstream * gate_two
     feed_gathered = gather_rows(feed_grad.astype(jnp.bfloat16))
-    reduce_total = contract_first(hidden_rows, feed_gathered)
-    hidden_grad = contract_last(feed_gathered, reduce_back) * hidden_slope
+    reduce_total = contract_first(feed_gathered, hidden_rows)
+    hidden_grad = jnp.dot(feed_gathered, reduce_full, preferred_element_type=jnp.float32) * hidden_slope
     hidden_round = hidden_grad.astype(jnp.bfloat16)
     expand_total = contract_first(feed_input, hidden_round)
-    feed_input_grad = sum_rows(contract_last(hidden_round, expand_back))
+    feed_input_grad = sum_rows(contract_last(hidden_round, expand_full))
     middle_grad = upstream + norm_back(feed_input_grad * (1.0 + scale_two), normed_two, inverse_two)
     attention_grad = middle_grad * gate_one
     attention_gathered = gather_rows(attention_grad.astype(jnp.bfloat16))
-    output_total = contract_first(attended, attention_gathered)
+    output_total = contract_first(attention_gathered, attended)
     attended_grad = (
-        contract_last(attention_gathered, output_back).astype(jnp.bfloat16).reshape(head_shape)
+        jnp.dot(attention_gathered, output_full, preferred_element_type=jnp.float32)
+        .astype(jnp.bfloat16)
+        .reshape(head_shape)
     )
     query_grad, key_grad, value_grad = attend_back(
         query_rows, key_rows, value_rows, log_total, attended_grad
@@ -213,8 +223,8 @@
         .astype(jnp.bfloat16)
         .reshape(group_rows, 3 * local_width)
     )
-    entry_total = contract_first(attention_input, entry_round).reshape(features, 3, local_width)
-    input_grad = sum_rows(contract_last(entry_round, entry_back.reshape(features, 3 * local_width)))
+    entry_total = contract_first(attention_input, entry_round)
+    input_grad = sum_rows(contract_last(entry_round, entry_full))
     tokens_gradient = middle_grad + norm_back(
         input_grad * (1.0 + scale_one), normed_one, inverse_one
     )
@@ -239,55 +249,47 @@
     modulation_grad = lax.psum_scatter(
         per_sequence.astype(jnp.bfloat16), "tensor", scatter_dimension=2, tiled=True
     ).astype(jnp.float32)
-    modulation_round = modulation_grad.astype(jnp.bfloat16).reshape(seq_count, 6 * local_width)
-    adaptive_total = contract_first(soft_condition, modulation_round).reshape(
-        features, 6, local_width
-    )
-    condition_partial = contract_last(
-        modulation_round, adaptive_back.reshape(features, 6 * local_width)
-    )
-    condition_sum = lax.psum(condition_partial, "tensor")
+    modulation_all = lax.all_gather(
+        modulation_grad.reshape(seq_count, 6 * local_width), "dp", axis=0, tiled=True
+    )
+    bias_adaptive = jnp.sum(modulation_all, axis=0).reshape(6, local_width)
+    modulation_round = modulation_all.astype(jnp.bfloat16)
+    adaptive_gradient = contract_first(soft_mine, modulation_round).reshape(
+        shard_rows, 6, local_width
+    )
+    condition_partial = contract_last(modulation_round, adaptive_flat)
+    condition_moved = lax.all_to_all(
+        condition_partial.reshape(dp_count, seq_count, shard_rows), "dp", 0, 0
+    )
+    condition_sum = lax.psum(
+        condition_moved.transpose(1, 0, 2).reshape(seq_count, features), "tensor"
+    )
     sigmoid_value = jax.nn.sigmoid(condition_float)
     condition_gradient = (
         condition_sum * sigmoid_value * (1.0 + condition_float * (1.0 - sigmoid_value))
     )
-    adaptive_gradient, entry_gradient, output_gradient, expand_gradient, reduce_gradient = (
-        lax.psum_scatter(adaptive_total, "dp", scatter_dimension=0, tiled=True),
-        lax.psum_scatter(entry_total, "dp", scatter_dimension=0, tiled=True),
-        lax.psum_scatter(output_total, "dp", scatter_dimension=1, tiled=True),
-        lax.psum_scatter(expand_total, "dp", scatter_dimension=0, tiled=True),
-        lax.psum_scatter(reduce_total, "dp", scatter_dimension=1, tiled=True),
-    )
-    width_start = tensor_index * local_width
-    hidden_start = tensor_index * local_hidden
-    adaptive_slot = lax.dynamic_update_slice_in_dim(
-        jnp.zeros((6, features), jnp.float32), jnp.sum(modulation_grad, axis=0), width_start, 1
-    )
-    entry_slot = lax.dynamic_update_slice_in_dim(
-        jnp.zeros((2, features), jnp.float32),
-        jnp.stack([jnp.sum(query_grad, axis=0), jnp.sum(value_grad, axis=0)]),
-        width_start,
-        1,
-    )
-    expand_slot = lax.dynamic_update_slice_in_dim(
-        jnp.zeros((local_hidden * tensor_count,), jnp.float32),
-        jnp.sum(hidden_grad, axis=0),
-        hidden_start,
-        0,
-    )
-    adaptive_sums, entry_sums, output_sums, expand_sums, reduce_sums = lax.psum(
-        (
-            adaptive_slot,
-            entry_slot,
+    entry_gradient, output_gradient, expand_gradient, reduce_gradient = scatter_gradients(
+        (entry_total, output_total, expand_total, reduce_total)
+    )
+    entry_gradient = entry_gradient.reshape(shard_rows, 3, local_width)
+    output_gradient = output_gradient.T
+    reduce_gradient = reduce_gradient.T
+    own_sums = jnp.concatenate(
+        [
+            jnp.sum(query_grad, axis=0),
+            jnp.sum(value_grad, axis=0),
+            jnp.sum(hidden_grad, axis=0),
             jnp.sum(attention_grad, axis=0),
-            expand_slot,
             jnp.sum(feed_grad, axis=0),
-        ),
-        ("dp", "tensor"),
-    )
-    bias_adaptive = lax.dynamic_slice_in_dim(adaptive_sums, width_start, local_width, 1)
-    bias_entry = lax.dynamic_slice_in_dim(entry_sums, width_start, local_width, 1)
-    bias_expand = lax.dynamic_slice_in_dim(expand_sums, hidden_start, local_hidden, 0)
+        ]
+    )
+    dp_sums = lax.psum(own_sums, "dp")
+    own_width = 2 * local_width + local_hidden
+    bias_entry = dp_sums[: 2 * local_width].reshape(2, local_width)
+    bias_expand = dp_sums[2 * local_width : own_width]
+    row_sums = lax.psum(dp_sums[own_width:], "tensor")
+    output_sums = row_sums[:features]
+    reduce_sums = row_sums[features:]
     return (
         block_output,
         tokens_gradient,

time: 775 us -> 676 us (0.87)
  waiting for transfers between devices: 471 us -> 322 us
  blocking collectives: 165 us -> 217 us
    reduce_scatter x4, waiting for transfers between devices: 260 us -> 175 us  [scatter_gradients(): lax.psum_scatter(total.astype(jnp.bfloat16), 'dp', scatter_dimension=0, t...]
    unnamed x15 -> x14, waiting for transfers between devices: 62.1 us -> 1.68 us
    all_gather x2 -> x4, blocking collectives: 73.4 us -> 129 us  [the longest x2 65.6 us: gather_weights(): return [lax.all_gather(shard, 'dp', axis=0, tiled=True) for shard in shards]]
    unnamed x99 -> x108, local copies, waits for them, and re-layouts: 14.4 us -> 15.8 us
    all_gather x3 -> x2, waiting for transfers between devices: 62.6 us -> 62.6 us  [gather_weights(): return [lax.all_gather(shard, 'dp', axis=0, tiled=True) for shard in shards]]
  transfers between devices with their start and end apart: 13 -> 13, of which waited for: 12 -> 11; matrix products, arithmetic and copies ran while one was open for 6% -> 9% of each run, Pallas kernels for 0% -> 0%
where the time goes in v1:
time: 676 us; the launch traced here: 674 us
  waiting for transfers between devices  322 us (48%)
  blocking collectives  217 us (32%)
  matrix products  53.9 us (8%)
  local copies, waits for them, and re-layouts  38.6 us (6%)
  other arithmetic  23.7 us (4%)
  between operations  15.4 us (2%)
    reduce_scatter x4, waiting for transfers between devices, scatter_gradients(): lax.psum_scatter(total.astype(jnp.bfloat16), 'dp', scatter_dimension=0, t...  175 us
    reduce_scatter x4, waiting for transfers between devices, sum_rows(): lax.psum_scatter(values.astype(jnp.bfloat16), 'tensor', scatter_dimension...  79.2 us
    all_gather x2, blocking collectives, gather_weights(): return [lax.all_gather(shard, 'dp', axis=0, tiled=True) for shard in shards]  65.6 us
    all_gather x2, waiting for transfers between devices, gather_weights(): return [lax.all_gather(shard, 'dp', axis=0, tiled=True) for shard in shards]  62.6 us
    psum x1, blocking collectives, body(): dp_sums = lax.psum(own_sums, 'dp')  35 us
    all_gather x4, blocking collectives, gather_rows(): return lax.all_gather(values, 'tensor', axis=0, tiled=True)  34.5 us
    all_gather x1, blocking collectives, body(): condition_all = lax.all_gather(condition, 'dp', axis=0, tiled=True)  32.6 us
    all_gather x1, blocking collectives, body(): lax.all_gather(modulation_grad.reshape(seq_count, 6 * local_width), 'dp',...  30.7 us
  transfers between devices with their start and end apart: 13, of which 11 were waited for; matrix products, arithmetic and copies ran while one was open for 9% of the time, Pallas kernels for 0%

profile of v1, /device:TPU:0, one launch (start us, length us, event | category | flops | bytes accessed | tf_op | source)
XLA Modules:
  0.0 674.4 jit_solution(6162113306208221612)
XLA Ops:
  7.3 32.6 %all-gather = bf16[8,2,768]{2,1,0:T(2,128)(2,1)S(1)} all-gather(bf16[1,2,768]{2,1,0:T(2,128)(2,1)} %bitcast.191), channel_id=1, replica_groups=mesh['dp'=8,'tensor'=4] {'dp'}, dimensions={0}, use_global_device_ids=true | all-gather | bytes 27648 | tf_op jit(solution)/shard_map/all_gather | solution.py:147
  44.9 33.2 %all_gather.37 = bf16[768,192]{1,0:T(8,128)(2,1)} all-gather(bf16[96,192]{1,0:T(8,128)(2,1)S(1)} %bitcast.187), channel_id=1, replica_groups=mesh['dp'=8,'tensor'=4] {'dp'}, dimensions={0}, use_global_device_ids=true | all-gather | bytes 331776 | tf_op jit(solution)/shard_map/all_gather | solution.py:62
  78.1 32.4 %all_gather.36 = bf16[768,576]{1,0:T(8,128)(2,1)S(1)} all-gather(bf16[96,576]{1,0:T(8,128)(2,1)S(1)} %copy.134), channel_id=1, replica_groups=mesh['dp'=8,'tensor'=4] {'dp'}, dimensions={0}, use_global_device_ids=true | all-gather | bytes 995328 | tf_op jit(solution)/shard_map/all_gather | solution.py:62
  113.7 8.4 %all_gather.34 = f32[2,6,768]{1,0,2:T(2,128)S(1)} all-gather(f32[2,6,192]{1,0,2:T(2,128)S(1)} %copy.131), channel_id=1, replica_groups=mesh['dp'=8,'tensor'=4] {'tensor'}, dimensions={2}, use_global_device_ids=true | all-gather | bytes 46080 | tf_op jit(solution)/shard_map/all_gather | solution.py:158
  123.1 2.0 fusion.90
  125.3 8.7 %all_gather.35 = bf16[512,768]{1,0:T(8,128)(2,1)S(1)} all-gather(bf16[128,768]{1,0:T(8,128)(2,1)S(1)} %fusion.44), channel_id=1, replica_groups=mesh['dp'=8,'tensor'=4] {'tensor'}, dimensions={0}, use_global_device_ids=true | all-gather | bytes 983040 | tf_op jit(solution)/shard_map/all_gather | solution.py:52
  142.6 22.5 %reduce-scatter.12.cloned.1.call-done = bf16[128,768]{1,0:T(8,128)(2,1)} async-done(((bf16[512,768]{1,0:T(8,128)(2,1)}), bf16[128,768]{1,0:T(8,128)(2,1)}) %reduce-scatter.12.cloned.1.call-update) | async-done | bytes 196624 | tf_op jit(solution)/shard_map/reduce_scatter | solution.py:56
  166.7 8.5 %all_gather.41 = bf16[512,768]{1,0:T(8,128)(2,1)} all-gather(bf16[128,768]{1,0:T(8,128)(2,1)S(1)} %get-tuple-element.95), channel_id=1, replica_groups=mesh['dp'=8,'tensor'=4] {'tensor'}, dimensions={0}, use_global_device_ids=true | all-gather | bytes 983040 | tf_op jit(solution)/shard_map/all_gather | solution.py:52
  175.2 9.1 %all_gather.38 = bf16[512,768]{1,0:T(8,128)(2,1)} all-gather(bf16[128,768]{1,0:T(8,128)(2,1)S(1)} %get-tuple-element.96), channel_id=1, replica_groups=mesh['dp'=8,'tensor'=4] {'tensor'}, dimensions={0}, use_global_device_ids=true | all-gather | bytes 983040 | tf_op jit(solution)/shard_map/all_gather | solution.py:52
  184.3 24.2 %all-gather.5.cloned.1.call-done = bf16[768,768]{1,0:T(8,128)(2,1)} async-done(((bf16[96,768]{1,0:T(8,128)(2,1)}), bf16[768,768]{1,0:T(8,128)(2,1)}) %all-gather.5.cloned.1.call-update) | async-done | bytes 1179664 | tf_op jit(solution)/shard_map/all_gather | solution.py:62
  208.5 3.4 convolution_add_fusion
  211.9 38.4 %all-gather.7.cloned.1.call-done = bf16[768,768]{1,0:T(8,128)(2,1)} async-done(((bf16[96,768]{1,0:T(8,128)(2,1)}), bf16[768,768]{1,0:T(8,128)(2,1)}) %all-gather.7.cloned.1.call-update) | async-done | bytes 1179664 | tf_op jit(solution)/shard_map/all_gather | solution.py:62
  250.4 4.1 fusion.108
  255.5 1.7 convolution_convert_fusion.3
  257.3 3.7 convolution_convert_fusion.4
  261.1 18.2 %reduce-scatter.16.cloned.1.call-done = bf16[128,768]{1,0:T(8,128)(2,1)} async-done(((bf16[512,768]{1,0:T(8,128)(2,1)}), bf16[128,768]{1,0:T(8,128)(2,1)}) %reduce-scatter.16.cloned.1.call-update) | async-done | bytes 196624 | tf_op jit(solution)/shard_map/reduce_scatter | solution.py:56
  280.9 24.0 %reduce-scatter.14.cloned.1.call-done = bf16[128,768]{1,0:T(8,128)(2,1)} async-done(((bf16[512,768]{1,0:T(8,128)(2,1)}), bf16[128,768]{1,0:T(8,128)(2,1)}) %reduce-scatter.14.cloned.1.call-update) | async-done | bytes 196624 | tf_op jit(solution)/shard_map/reduce_scatter | solution.py:56
  304.9 2.0 fusion.77
  306.9 8.2 %all_gather.42 = bf16[512,768]{1,0:T(8,128)(2,1)S(1)} all-gather(bf16[128,768]{1,0:T(8,128)(2,1)S(1)} %get-tuple-element.90), channel_id=1, replica_groups=mesh['dp'=8,'tensor'=4] {'tensor'}, dimensions={0}, use_global_device_ids=true | all-gather | bytes 983040 | tf_op jit(solution)/shard_map/all_gather | solution.py:52
  318.0 3.1 fusion.102
  322.8 4.4 fusion.25
  327.2 4.8 fusion.103
  332.0 1.8 copy.149
  334.9 1.8 copy.146
  336.7 1.7 stack_reshape.13
  338.4 1.8 copy.144
  340.2 1.7 stack_reshape.12
  343.9 3.0 convolution_convert_fusion.5
  346.9 2.3 convolution_convert_fusion.7
  349.3 3.6 convolution_convert_fusion
  353.0 3.2 convolution_convert_fusion.1
  356.3 14.5 %reduce-scatter.18.cloned.1.call-done = bf16[128,768]{1,0:T(8,128)(2,1)} async-done(((bf16[512,768]{1,0:T(8,128)(2,1)}), bf16[128,768]{1,0:T(8,128)(2,1)}) %reduce-scatter.18.cloned.1.call-update) | async-done | bytes 196624 | tf_op jit(solution)/shard_map/reduce_scatter | solution.py:56
  370.8 1.7 fusion.55
  372.6 1.9 fusion.57
  374.5 1.7 bitcast_dynamic-update-slice_fusion
  379.4 3.1 copy.150
  382.4 2.8 fusion.28
  385.2 1.9 copy.169
  387.1 2.7 reshape.219
  390.0 3.1 convolution_convert_fusion.2
  393.3 43.7 %reduce-scatter.22.cloned.1.call-done = bf16[96,192]{1,0:T(8,128)(2,1)} async-done(((bf16[768,192]{1,0:T(8,128)(2,1)}), bf16[96,192]{1,0:T(8,128)(2,1)}) %reduce-scatter.22.cloned.1.call-update) | async-done | bytes 36880 | tf_op jit(solution)/shard_map/reduce_scatter | solution.py:67
  438.5 65.6 %reduce-scatter.26.cloned.1.call-done = bf16[96,768]{1,0:T(8,128)(2,1)} async-done(((bf16[768,768]{1,0:T(8,128)(2,1)}), bf16[96,768]{1,0:T(8,128)(2,1)}) %reduce-scatter.26.cloned.1.call-update) | async-done | bytes 147472 | tf_op jit(solution)/shard_map/reduce_scatter | solution.py:67
  505.7 65.3 %reduce-scatter.24.cloned.1.call-done = bf16[96,768]{1,0:T(8,128)(2,1)} async-done(((bf16[768,768]{1,0:T(8,128)(2,1)}), bf16[96,768]{1,0:T(8,128)(2,1)}) %reduce-scatter.24.cloned.1.call-update) | async-done | bytes 147472 | tf_op jit(solution)/shard_map/reduce_scatter | solution.py:67
  573.0 35.0 %psum.22 = f32[2688]{0:T(1024)S(1)} all-reduce(f32[2688]{0:T(1024)S(1)} %concatenate.3), channel_id=1, replica_groups=mesh['dp'=8,'tensor'=4] {'dp'}, use_global_device_ids=true, to_apply=%region_25.26 | all-reduce | flops 2688 | bytes 21504 | tf_op jit(solution)/shard_map/psum | solution.py:286
  611.5 30.7 %all-gather.1 = f32[8,2,1152]{2,1,0:T(2,128)S(1)} all-gather(f32[1,2,1152]{2,1,0:T(2,128)S(1)} %reshape.211), channel_id=1, replica_groups=mesh['dp'=8,'tensor'=4] {'dp'}, dimensions={0}, use_global_device_ids=true | all-gather | bytes 82944 | tf_op jit(solution)/shard_map/all_gather | solution.py:252
  644.1 3.3 all-to-all-start
  650.2 3.6 all-to-all-done
  653.9 10.5 %all-reduce.1 = (f32[2,768]{1,0:T(2,128)S(1)}, f32[1536]{0:T(1024)S(1)}) all-reduce(f32[2,768]{1,0:T(2,128)S(1)} %reshape.199, f32[1536]{0:T(1024)S(1)} %slice.83), channel_id=1, replica_groups=mesh['dp'=8,'tensor'=4] {'tensor'}, use_global_device_ids=true, to_apply=%region_17.18 | all-reduce | flops 3072 | bytes 24576 | tf_op jit(solution)/shard_map/psum | solution.py:264
  (204 shorter events, 49.2 us)
Async XLA Ops:
  7.2 37.1 %copy-start.42 = (f32[2,192]{1,0:T(2,128)S(1)}, f32[2,192]{1,0:T(2,128)}, u32[]{:S(2)}) copy-start(f32[2,192]{1,0:T(2,128)} %param.18) | copy-start | bytes 4612
  7.2 37.3 %copy-start.24 = (bf16[192,96]{1,0:T(8,128)(2,1)S(1)}, bf16[192,96]{1,0:T(8,128)(2,1)}, u32[]{:S(2)}) copy-start(bf16[192,96]{1,0:T(8,128)(2,1)} %param.19) | copy-start | bytes 110596
  7.2 37.4 %copy-start.22 = (bf16[96,3,192]{2,0,1:T(8,128)(2,1)S(1)}, bf16[96,3,192]{2,0,1:T(8,128)(2,1)}, u32[]{:S(2)}) copy-start(bf16[96,3,192]{2,0,1:T(8,128)(2,1)} %param.17) | copy-start | bytes 331780
  7.2 105.5 %all-reduce.4.cloned.1.call-start = ((), (), s32[]{:S(2)}) async-start(), calls=%async_computation.21 | async-start | bytes 147456
  39.9 4.6 copy-start.23
  41.1 72.5 %copy-start.14 = (bf16[96,6,192]{0,2,1:T(8,128)(2,1)}, bf16[96,6,192]{0,2,1:T(8,128)(2,1)S(1)}, u32[]{:S(2)}) copy-start(bf16[96,6,192]{0,2,1:T(8,128)(2,1)S(1)} %copy.130) | copy-start | bytes 663556
  41.1 69.4 %copy-start.45 = (u32[32]{0:T(128)S(1)}, u32[32]{0:T(128)}, u32[]{:S(2)}) copy-start(u32[32]{0:T(128)} %constant.67) | copy-start | bytes 388
  41.1 72.4 %copy-start.37 = (f32[6,192]{1,0:T(8,128)S(1)}, f32[6,192]{1,0:T(8,128)}, u32[]{:S(2)}) copy-start(f32[6,192]{1,0:T(8,128)} %param.16) | copy-start | bytes 13828
  42.0 123.1 %reduce-scatter.12.cloned.1.call-start = ((), (), s32[]{:S(2)}) async-start(), calls=%async_computation.10 | async-start | bytes 983040 | tf_op jit(solution)/shard_map/reduce_scatter | solution.py:56
  43.1 81.9 %copy-start.27 = (f32[128]{0:T(128)}, f32[128]{0:T(128)S(1)}, u32[]{:S(2)}) copy-start(f32[128]{0:T(128)S(1)} %broadcast_multiply_fusion.5) | copy-start | bytes 1540
  44.3 80.8 %copy-start.33 = (f32[128]{0:T(128)}, f32[128]{0:T(128)S(1)}, u32[]{:S(2)}) copy-start(f32[128]{0:T(128)S(1)} %add_rsqrt_fusion.1) | copy-start | bytes 1540
  44.5 92.9 %copy-start.35 = (f32[3,64]{1,0:T(4,128)}, f32[3,64]{1,0:T(4,128)S(1)}, u32[]{:S(2)}) copy-start(f32[3,64]{1,0:T(4,128)S(1)} %add.190) | copy-start | bytes 2308
  110.5 23.5 %copy-start.3 = (bf16[768,576]{1,0:T(8,128)(2,1)}, bf16[768,576]{1,0:T(8,128)(2,1)S(1)}, u32[]{:S(2)}) copy-start(bf16[768,576]{1,0:T(8,128)(2,1)S(1)} %all_gather.36) | copy-start | bytes 2654212
  139.0 26.1 %copy-start.25 = (f32[768]{0:T(1024)S(1)}, f32[768]{0:T(1024)}, u32[]{:S(2)}) copy-start(f32[768]{0:T(1024)} %param.20) | copy-start | bytes 9220
  141.3 25.2 %copy-start.11 = (bf16[128,768]{1,0:T(8,128)(2,1)S(1)}, bf16[128,768]{1,0:T(8,128)(2,1)}, u32[]{:S(2)}) copy-start(bf16[128,768]{1,0:T(8,128)(2,1)} %param.25) | copy-start | bytes 589828
  141.3 67.2 %all-gather.5.cloned.1.call-start = ((), (), s32[]{:S(2)}) async-start(), calls=%async_computation.11 | async-start | bytes 1327104 | tf_op jit(solution)/shard_map/all_gather | solution.py:62
  142.0 108.4 %all-gather.7.cloned.1.call-start = ((), (), s32[]{:S(2)}) async-start(), calls=%async_computation.12 | async-start | bytes 1327104 | tf_op jit(solution)/shard_map/all_gather | solution.py:62
  142.6 136.6 %reduce-scatter.16.cloned.1.call-start = ((), (), s32[]{:S(2)}) async-start(), calls=%async_computation.14 | async-start | bytes 983040 | tf_op jit(solution)/shard_map/reduce_scatter | solution.py:56
  166.3 8.9 %copy-start.29 = (f32[128]{0:T(128)}, f32[128]{0:T(128)S(1)}, u32[]{:S(2)}) copy-start(f32[128]{0:T(128)S(1)} %broadcast_multiply_fusion.4) | copy-start | bytes 1540
  166.5 8.7 %copy-start.38 = (f32[128]{0:T(128)}, f32[128]{0:T(128)S(1)}, u32[]{:S(2)}) copy-start(f32[128]{0:T(128)S(1)} %add_rsqrt_fusion) | copy-start | bytes 1540
  250.4 5.1 copy-start.44
  257.2 22.0 %copy-start.30 = (f32[128]{0:T(128)S(1)}, f32[128]{0:T(128)}, u32[]{:S(2)}) copy-start(f32[128]{0:T(128)} %copy-done.29) | copy-start | bytes 1540
  257.2 22.0 %copy-start.39 = (f32[128]{0:T(128)S(1)}, f32[128]{0:T(128)}, u32[]{:S(2)}) copy-start(f32[128]{0:T(128)} %copy-done.38) | copy-start | bytes 1540
  257.2 47.7 %reduce-scatter.14.cloned.1.call-start = ((), (), s32[]{:S(2)}) async-start(), calls=%async_computation.13 | async-start | bytes 983040 | tf_op jit(solution)/shard_map/reduce_scatter | solution.py:56
  261.0 109.8 %reduce-scatter.18.cloned.1.call-start = ((), (), s32[]{:S(2)}) async-start(), calls=%async_computation.15 | async-start | bytes 983040 | tf_op jit(solution)/shard_map/reduce_scatter | solution.py:56
  304.9 11.1 %copy-start.7 = (bf16[768,192]{1,0:T(8,128)(2,1)S(1)}, bf16[768,192]{1,0:T(8,128)(2,1)}, u32[]{:S(2)}) copy-start(bf16[768,192]{1,0:T(8,128)(2,1)} %all_gather.37) | copy-start | bytes 884740
  318.0 3.1 copy-start.5
  322.8 4.4 copy-start.19
  346.9 90.0 %reduce-scatter.22.cloned.1.call-start = ((), (), s32[]{:S(2)}) async-start(), calls=%async_computation.17 | async-start | bytes 442368 | tf_op jit(solution)/shard_map/reduce_scatter | solution.py:67
  349.3 154.8 %reduce-scatter.26.cloned.1.call-start = ((), (), s32[]{:S(2)}) async-start(), calls=%async_computation.19 | async-start | bytes 1327104 | tf_op jit(solution)/shard_map/reduce_scatter | solution.py:67
  353.0 218.0 %reduce-scatter.24.cloned.1.call-start = ((), (), s32[]{:S(2)}) async-start(), calls=%async_computation.18 | async-start | bytes 1327104 | tf_op jit(solution)/shard_map/reduce_scatter | solution.py:67
  356.2 16.3 %copy-start.28 = (f32[128]{0:T(128)S(1)}, f32[128]{0:T(128)}, u32[]{:S(2)}) copy-start(f32[128]{0:T(128)} %copy-done.27) | copy-start | bytes 1540
  356.2 19.9 %copy-start.10 = (bf16[128,768]{1,0:T(8,128)(2,1)S(1)}, bf16[128,768]{1,0:T(8,128)(2,1)}, u32[]{:S(2)}) copy-start(bf16[128,768]{1,0:T(8,128)(2,1)} %reduce-scatter.16.cloned.1.call-done) | copy-start | bytes 589828
  356.3 20.7 %copy-start.31 = (f32[128]{0:T(128)S(1)}, f32[128]{0:T(128)}, u32[]{:S(2)}) copy-start(f32[128]{0:T(128)} %copy-done.29) | copy-start | bytes 1540
  356.3 253.8 %reduce-scatter.28.cloned.1.call-start = ((), (), s32[]{:S(2)}) async-start(), calls=%async_computation.20 | async-start | bytes 245760
  372.5 6.0 copy-start.12
  372.5 6.0 copy-start.20
  372.5 6.0 copy-start.26
  379.4 3.1 copy-start.43
  389.9 3.2 copy-start.36
  389.9 3.3 copy-start.41
  389.9 275.8 %reduce-scatter.20.cloned.1.call-start = ((), (), s32[]{:S(2)}) async-start(), calls=%async_computation.16 | async-start | bytes 1105920 | tf_op jit(solution)/shard_map/reduce_scatter | solution.py:67
  393.1 179.6 %copy-start.8 = (bf16[128,768]{1,0:T(8,128)(2,1)S(1)}, bf16[128,768]{1,0:T(8,128)(2,1)}, u32[]{:S(2)}) copy-start(bf16[128,768]{1,0:T(8,128)(2,1)} %reduce-scatter.18.cloned.1.call-done) | copy-start | bytes 589828
  393.1 179.6 %copy-start.13 = (bf16[128,768]{1,0:T(8,128)(2,1)S(1)}, bf16[128,768]{1,0:T(8,128)(2,1)}, u32[]{:S(2)}) copy-start(bf16[128,768]{1,0:T(8,128)(2,1)} %param.25) | copy-start | bytes 589828
  393.1 179.6 %copy-start.34 = (f32[128]{0:T(128)S(1)}, f32[128]{0:T(128)}, u32[]{:S(2)}) copy-start(f32[128]{0:T(128)} %copy-done.33) | copy-start | bytes 1540
  438.5 134.4 %copy-start.40 = (f32[768]{0:T(1024)S(1)}, f32[768]{0:T(1024)}, u32[]{:S(2)}) copy-start(f32[768]{0:T(1024)} %get-tuple-element.109) | copy-start | bytes 9220
  611.2 53.9 %copy-start.32 = (bf16[2,768]{1,0:T(2,128)(2,1)S(1)}, bf16[2,768]{1,0:T(2,128)(2,1)}, u32[]{:S(2)}) copy-start(bf16[2,768]{1,0:T(2,128)(2,1)} %param.14) | copy-start | bytes 9220
  644.1 9.8 %all-to-all-start = ((f32[8,2,96]{2,1,0:T(2,128)}), f32[8,2,96]{2,1,0:T(2,128)S(1)}, u32[]{:S(2)}, u32[]{:S(2)}) async-start(f32[8,2,96]{2,1,0:T(2,128)} %copy.154), calls=%async_computation.4 | async-start | bytes 16384 | tf_op jit(solution)/shard_map/all_to_all | solution.py:261
  (12 other events, 18.3 us)
Sparse Core Ops, SparseCore 0:
  42.2 70.4 all-reduce.3
  141.4 23.7 reduce-scatter.11
  167.4 41.0 all-gather.4
  210.5 39.8 all-gather.6
  257.3 21.8 reduce-scatter.15
  281.6 23.2 reduce-scatter.13
  347.0 23.7 reduce-scatter.17
  374.7 62.1 reduce-scatter.21
  440.3 63.6 reduce-scatter.25
  507.3 63.6 reduce-scatter.23
  573.4 18.8 reduce-scatter.27
  595.5 64.1 reduce-scatter.19

commit v2 on v1

--- a/solution.py
+++ b/solution.py
@@ -1,6 +1,10 @@
+import functools
+
 import jax
 import jax.numpy as jnp
 from jax import lax
+from jax.experimental import pallas as pl
+from jax.experimental.pallas import tpu as pltpu
 from jax.sharding import PartitionSpec as P
 
 HEAD_DIM = 64
@@ -58,17 +62,243 @@
     ).astype(jnp.float32)
 
 
+MESH = pl.DeviceIdType.MESH
+ANY = pl.BlockSpec(memory_space=pl.ANY)
+VMEM = pl.BlockSpec(memory_space=pltpu.VMEM)
+PAIR = 2
+
+
+def greet(position, length, mate, below, above):
+    barrier = pltpu.get_barrier_semaphore()
+    pl.semaphore_signal(barrier, inc=1, device_id=mate, device_id_type=MESH)
+
+    @pl.when(position > 0)
+    def _():
+        pl.semaphore_signal(barrier, inc=1, device_id=below, device_id_type=MESH)
+
+    @pl.when(position < length - 1)
+    def _():
+        pl.semaphore_signal(barrier, inc=1, device_id=above, device_id_type=MESH)
+
+    inner = jnp.minimum(position, 1) + jnp.minimum(length - 1 - position, 1)
+    pl.semaphore_wait(barrier, 1 + inner)
+
+
+def places(length):
+    me = lax.axis_index("dp")
+    column = lax.axis_index("tensor")
+    position, side = me // PAIR, me % PAIR
+    mate = (position * PAIR + 1 - side, column)
+    below = (jnp.maximum(me - PAIR, 0), column)
+    above = (jnp.minimum(me + PAIR, length * PAIR - 1), column)
+    return position, side, mate, below, above
+
+
+def gather_kernel(length, count, *refs):
+    ins, outs = refs[:count], refs[count : 2 * count]
+    own_sem, send_sem, recv_sem = refs[2 * count :]
+    position, side, mate, below, above = places(length)
+    greet(position, length, mate, below, above)
+
+    def copy(way, item, shard, target, source=None):
+        place = outs[item].at[shard * PAIR + side]
+        return pltpu.make_async_remote_copy(
+            src_ref=place if source is None else source,
+            dst_ref=place,
+            send_sem=send_sem.at[way, item, shard],
+            recv_sem=recv_sem.at[way, item, shard],
+            device_id=target,
+            device_id_type=MESH,
+        )
+
+    def own(item):
+        return pltpu.make_async_copy(
+            ins[item], outs[item].at[position * PAIR + side], own_sem.at[item]
+        )
+
+    for item in range(count):
+        own(item).start()
+    for step in range(length):
+        for item in range(count):
+            source = ins[item] if step == 0 else None
+            low = position - step
+            high = position + step
+
+            @pl.when(low >= 0)
+            def _(item=item, low=low, source=source, step=step):
+                if step > 0:
+                    copy(0, item, low, above).wait_recv()
+
+                @pl.when(position < length - 1)
+                def _():
+                    copy(0, item, low, above, source).start()
+
+                copy(2, item, low, mate, source).start()
+
+            @pl.when(high < length)
+            def _(item=item, high=high, source=source, step=step):
+                if step > 0:
+                    copy(1, item, high, below).wait_recv()
+
+                @pl.when(position > 0)
+                def _():
+                    copy(1, item, high, below, source).start()
+
+                if step > 0:
+                    copy(2, item, high, mate).start()
+
+    for item in range(count):
+        own(item).wait()
+        for shard in range(length):
+            place = outs[item].at[shard * PAIR + 1 - side]
+            pltpu.make_async_remote_copy(
+                src_ref=place,
+                dst_ref=place,
+                send_sem=send_sem.at[2, item, shard],
+                recv_sem=recv_sem.at[2, item, shard],
+                device_id=mate,
+                device_id_type=MESH,
+            ).wait_recv()
+            copy(2, item, shard, mate).wait_send()
+
+            @pl.when((shard <= position) & (position < length - 1))
+            def _(item=item, shard=shard):
+                copy(0, item, shard, above).wait_send()
+
+            @pl.when((shard >= position) & (position > 0))
+            def _(item=item, shard=shard):
+                copy(1, item, shard, below).wait_send()
+
+
 def gather_weights(shards):
-    return [lax.all_gather(shard, "dp", axis=0, tiled=True) for shard in shards]
+    dp_count = lax.axis_size("dp")
+    length, count = dp_count // PAIR, len(shards)
+    gathered = pl.pallas_call(
+        functools.partial(gather_kernel, length, count),
+        out_shape=[jax.ShapeDtypeStruct((dp_count,) + s.shape, s.dtype) for s in shards],
+        in_specs=[ANY] * count,
+        out_specs=[ANY] * count,
+        scratch_shapes=[
+            pltpu.SemaphoreType.DMA((count,)),
+            pltpu.SemaphoreType.DMA((3, count, length)),
+            pltpu.SemaphoreType.DMA((3, count, length)),
+        ],
+        compiler_params=pltpu.CompilerParams(collective_id=0, has_side_effects=True),
+    )(*shards)
+    return [g.reshape(dp_count * g.shape[1], g.shape[2]) for g in gathered]
+
+
+def scatter_kernel(length, count, *refs):
+    ins, outs = refs[:count], refs[count : 2 * count]
+    swap_refs = refs[2 * count : 3 * count]
+    sent_refs = refs[3 * count : 4 * count]
+    line_refs = refs[4 * count : 5 * count]
+    send_sem, recv_sem = refs[5 * count :]
+    position, side, mate, below, above = places(length)
+    greet(position, length, mate, below, above)
+    order = []
+    for step in range(length):
+        for target in (length - 1 - step, step):
+            if target not in order:
+                order.append(target)
+
+    def swap(item, target):
+        return pltpu.make_async_remote_copy(
+            src_ref=ins[item].at[target * PAIR + 1 - side],
+            dst_ref=swap_refs[item].at[target],
+            send_sem=send_sem.at[2, item, target],
+            recv_sem=recv_sem.at[2, item, target],
+            device_id=mate,
+            device_id_type=MESH,
+        )
+
+    def hop(way, item, target):
+        return pltpu.make_async_remote_copy(
+            src_ref=sent_refs[item].at[target],
+            dst_ref=line_refs[item].at[way, target],
+            send_sem=send_sem.at[way, item, target],
+            recv_sem=recv_sem.at[way, item, target],
+            device_id=above if way == 0 else below,
+            device_id_type=MESH,
+        )
+
+    def paired(item, target):
+        swap(item, target).wait_recv()
+        mine = ins[item][target * PAIR + side].astype(jnp.float32)
+        return mine + swap_refs[item][target].astype(jnp.float32)
+
+    for target in order:
+        for item in range(count):
+            swap(item, target).start()
+    for target in order:
+        for item in range(count):
+            for way, passes, inner in (
+                (0, position < target, position > 0),
+                (1, position > target, position < length - 1),
+            ):
+
+                @pl.when(passes)
+                def _(way=way, inner=inner, item=item, target=target):
+                    kind = sent_refs[item].dtype
+
+                    @pl.when(inner)
+                    def _():
+                        hop(way, item, target).wait_recv()
+                        total = paired(item, target) + line_refs[item][way, target].astype(
+                            jnp.float32
+                        )
+                        sent_refs[item][target] = total.astype(kind)
+
+                    @pl.when(jnp.logical_not(inner))
+                    def _():
+                        sent_refs[item][target] = paired(item, target).astype(kind)
+
+                    hop(way, item, target).start()
+
+    for item in range(count):
+        for target in range(length):
+
+            @pl.when(position == target)
+            def _(item=item, target=target):
+                outs[item][...] = paired(item, target)
+                if target > 0:
+                    hop(0, item, target).wait_recv()
+                    outs[item][...] += line_refs[item][0, target].astype(jnp.float32)
+                if target < length - 1:
+                    hop(1, item, target).wait_recv()
+                    outs[item][...] += line_refs[item][1, target].astype(jnp.float32)
+
+            @pl.when(position < target)
+            def _(item=item, target=target):
+                hop(0, item, target).wait_send()
+
+            @pl.when(position > target)
+            def _(item=item, target=target):
+                hop(1, item, target).wait_send()
+
+            swap(item, target).wait_send()
 
 
 def scatter_gradients(totals):
-    return [
-        lax.psum_scatter(
-            total.astype(jnp.bfloat16), "dp", scatter_dimension=0, tiled=True
-        ).astype(jnp.float32)
-        for total in totals
-    ]
+    dp_count = lax.axis_size("dp")
+    length, count = dp_count // PAIR, len(totals)
+    kind = jnp.bfloat16
+    parts = [t.astype(kind).reshape(dp_count, t.shape[0] // dp_count, t.shape[1]) for t in totals]
+    shapes = [p.shape[1:] for p in parts]
+    return pl.pallas_call(
+        functools.partial(scatter_kernel, length, count),
+        out_shape=[jax.ShapeDtypeStruct(s, jnp.float32) for s in shapes],
+        in_specs=[VMEM] * count,
+        out_specs=[VMEM] * count,
+        scratch_shapes=[pltpu.VMEM((length,) + s, kind) for s in shapes]
+        + [pltpu.VMEM((length,) + s, kind) for s in shapes]
+        + [pltpu.VMEM((2, length) + s, kind) for s in shapes]
+        + [
+            pltpu.SemaphoreType.DMA((3, count, length)),
+            pltpu.SemaphoreType.DMA((3, count, length)),
+        ],
+        compiler_params=pltpu.CompilerParams(collective_id=1, has_side_effects=True),
+    )(*parts)
 
 
 def attend(query_rows, key_rows, value_rows):

time: 676 us -> 472 us (0.70)
  waiting for transfers between devices: 322 us -> 95.5 us
  Pallas kernels: 0 us -> 88.9 us
  blocking collectives: 217 us -> 154 us
  local copies, waits for them, and re-layouts: 38.6 us -> 50.9 us
  matrix products: 53.9 us -> 43.7 us
    reduce_scatter x4 -> x0, waiting for transfers between devices: 175 us -> none  [scatter_gradients(): lax.psum_scatter(total.astype(jnp.bfloat16), 'dp', scatter_dimension=0, t...]
    pallas_call x0 -> x2, Pallas kernels: none -> 88.9 us  [the longest x1 51.1 us: scatter_gradients(): pl.pallas_call(functools.partial(scatter_kernel, length, count), out_shap...]
    all_gather x2 -> x0, blocking collectives: 65.6 us -> none  [gather_weights(): return [lax.all_gather(shard, 'dp', axis=0, tiled=True) for shard in shards]]
    all_gather x2 -> x0, waiting for transfers between devices: 62.6 us -> none  [gather_weights(): return [lax.all_gather(shard, 'dp', axis=0, tiled=True) for shard in shards]]
    unnamed x14 -> x8, waiting for transfers between devices: 1.68 us -> 25.7 us
    reduce_scatter x4, waiting for transfers between devices: 79.2 us -> 66.2 us  [sum_rows(): lax.psum_scatter(values.astype(jnp.bfloat16), 'tensor', scatter_dimension...]
    unnamed x108 -> x142, local copies, waits for them, and re-layouts: 15.8 us -> 20.5 us
  transfers between devices with their start and end apart: 13 -> 7, of which waited for: 11 -> 5; matrix products, arithmetic and copies ran while one was open for 9% -> 8% of each run, Pallas kernels for 0% -> 19%
where the time goes in v2:
time: 472 us; the launch traced here: 471 us
  blocking collectives  154 us (33%)
  waiting for transfers between devices  95.5 us (20%)
  Pallas kernels  88.9 us (19%)
  local copies, waits for them, and re-layouts  50.9 us (11%)
  matrix products  43.7 us (9%)
  other arithmetic  18.4 us (4%)
  between operations  15.5 us (3%)
    reduce_scatter x4, waiting for transfers between devices, sum_rows(): lax.psum_scatter(values.astype(jnp.bfloat16), 'tensor', scatter_dimension...  66.2 us
    pallas_call x1, Pallas kernels, scatter_gradients(): pl.pallas_call(functools.partial(scatter_kernel, length, count), out_shap...  51.1 us
    psum x1, blocking collectives, body(): dp_sums = lax.psum(own_sums, 'dp')  38.7 us
    pallas_call x1, Pallas kernels, gather_weights(): pl.pallas_call(functools.partial(gather_kernel, length, count), out_shape...  37.9 us
    all_gather x4, blocking collectives, gather_rows(): return lax.all_gather(values, 'tensor', axis=0, tiled=True)  33.6 us
    all_gather x1, blocking collectives, body(): condition_all = lax.all_gather(condition, 'dp', axis=0, tiled=True)  32.6 us
    all_gather x1, blocking collectives, body(): lax.all_gather(modulation_grad.reshape(seq_count, 6 * local_width), 'dp',...  30.5 us
    unnamed x8, waiting for transfers between devices  25.7 us
  transfers between devices with their start and end apart: 7, of which 5 were waited for; matrix products, arithmetic and copies ran while one was open for 8% of the time, Pallas kernels for 19%

profile of v2, /device:TPU:0, one launch (start us, length us, event | category | flops | bytes accessed | tf_op | source)
XLA Modules:
  0.0 470.8 jit_solution(2659386997527177228)
XLA Ops:
  7.3 32.6 %all-gather = bf16[8,2,768]{2,1,0:T(2,128)(2,1)S(1)} all-gather(bf16[1,2,768]{2,1,0:T(2,128)(2,1)} %bitcast.210), channel_id=1, replica_groups=mesh['dp'=8,'tensor'=4] {'dp'}, dimensions={0}, use_global_device_ids=true | all-gather | bytes 27648 | tf_op jit(solution)/shard_map/all_gather | solution.py:377
  46.2 37.9 %shard_map.228 = (bf16[8,96,576]{2,1,0:T(8,128)(2,1)}, bf16[8,96,192]{2,1,0:T(8,128)(2,1)}, bf16[8,96,768]{2,1,0:T(8,128)(2,1)}, bf16[8,96,768]{2,1,0:T(8,128)(2,1)}) custom-call(bf16[96,576]{1,0:T(8,128)(2,1)} %copy.114.refs_0_, bf16[96,192]{1,0:T(8,128)(2,1)} %bitcast.205, bf16[96,768]{1,0:T(8,128)(2,1)} %refs_2_.1, bf16[96,768]{1,0:T(8,128)(2,1)} %bitcast.207), custom_call_target="tpu_custom_call" | custom-call | tf_op jit(solution)/shard_map/pallas_call | solution.py:176
  84.1 1.5 copy.115
  86.9 25.6 %all-reduce.4.cloned.1.call-done = f32[16,1152]{1,0:T(8,128)} async-done(((f32[16,1152]{1,0:T(8,128)}), f32[16,1152]{1,0:T(8,128)}) %all-reduce.4.cloned.1.call-update) | async-done | bytes 73744
  113.5 8.6 %all_gather.22 = f32[2,6,768]{1,0,2:T(2,128)S(1)} all-gather(f32[2,6,192]{1,0,2:T(2,128)S(1)} %copy.110), channel_id=1, replica_groups=mesh['dp'=8,'tensor'=4] {'tensor'}, dimensions={2}, use_global_device_ids=true | all-gather | bytes 46080 | tf_op jit(solution)/shard_map/all_gather | solution.py:388
  123.9 8.7 %all_gather.23 = bf16[512,768]{1,0:T(8,128)(2,1)S(1)} all-gather(bf16[128,768]{1,0:T(8,128)(2,1)S(1)} %fusion.43), channel_id=1, replica_groups=mesh['dp'=8,'tensor'=4] {'tensor'}, dimensions={0}, use_global_device_ids=true | all-gather | bytes 983040 | tf_op jit(solution)/shard_map/all_gather | solution.py:56
  134.6 1.4 squeeze.24
  138.5 1.3 convolution_convert_fusion.6
  139.9 22.4 %reduce-scatter.8.cloned.1.call-done = bf16[128,768]{1,0:T(8,128)(2,1)} async-done(((bf16[512,768]{1,0:T(8,128)(2,1)}), bf16[128,768]{1,0:T(8,128)(2,1)}) %reduce-scatter.8.cloned.1.call-update) | async-done | bytes 196624 | tf_op jit(solution)/shard_map/reduce_scatter | solution.py:60
  163.8 8.1 %all_gather.25 = bf16[512,768]{1,0:T(8,128)(2,1)S(1)} all-gather(bf16[128,768]{1,0:T(8,128)(2,1)S(1)} %get-tuple-element.98), channel_id=1, replica_groups=mesh['dp'=8,'tensor'=4] {'tensor'}, dimensions={0}, use_global_device_ids=true | all-gather | bytes 983040 | tf_op jit(solution)/shard_map/all_gather | solution.py:56
  172.0 8.7 %all_gather.24 = bf16[512,768]{1,0:T(8,128)(2,1)S(1)} all-gather(bf16[128,768]{1,0:T(8,128)(2,1)S(1)} %get-tuple-element.99), channel_id=1, replica_groups=mesh['dp'=8,'tensor'=4] {'tensor'}, dimensions={0}, use_global_device_ids=true | all-gather | bytes 983040 | tf_op jit(solution)/shard_map/all_gather | solution.py:56
  182.2 2.0 fusion.107
  185.2 1.7 convolution_convert_fusion.3
  187.0 3.7 convolution_convert_fusion.4
  190.9 19.9 %reduce-scatter.12.cloned.1.call-done = bf16[128,768]{1,0:T(8,128)(2,1)} async-done(((bf16[512,768]{1,0:T(8,128)(2,1)}), bf16[128,768]{1,0:T(8,128)(2,1)}) %reduce-scatter.12.cloned.1.call-update) | async-done | bytes 196624 | tf_op jit(solution)/shard_map/reduce_scatter | solution.py:60
  212.5 24.0 %reduce-scatter.10.cloned.1.call-done = bf16[128,768]{1,0:T(8,128)(2,1)} async-done(((bf16[512,768]{1,0:T(8,128)(2,1)}), bf16[128,768]{1,0:T(8,128)(2,1)}) %reduce-scatter.10.cloned.1.call-update) | async-done | bytes 196624 | tf_op jit(solution)/shard_map/reduce_scatter | solution.py:60
  236.4 2.0 fusion.76
  238.4 8.0 %all_gather.26 = bf16[512,768]{1,0:T(8,128)(2,1)S(1)} all-gather(bf16[128,768]{1,0:T(8,128)(2,1)S(1)} %get-tuple-element.93), channel_id=1, replica_groups=mesh['dp'=8,'tensor'=4] {'tensor'}, dimensions={0}, use_global_device_ids=true | all-gather | bytes 983040 | tf_op jit(solution)/shard_map/all_gather | solution.py:56
  249.4 3.1 fusion.106
  252.5 1.6 fusion.71
  254.1 4.4 fusion.21
  258.6 4.3 fusion.103
  262.8 1.8 copy.129
  265.7 1.8 copy.126
  267.5 1.7 stack_reshape.10
  269.2 1.8 copy.124
  271.0 1.7 stack_reshape.9
  274.7 2.9 convolution_convert_fusion.5
  277.7 3.3 convolution_convert_fusion.1
  281.0 2.0 convolution_convert_fusion
  284.1 1.9 copy.139
  287.2 2.9 convolution_convert_fusion.2
  290.1 2.2 copy.138
  292.3 51.1 %shard_map.229 = (f32[96,576]{1,0:T(8,128)}, f32[96,192]{1,0:T(8,128)}, f32[96,768]{1,0:T(8,128)}, f32[96,768]{1,0:T(8,128)}) custom-call(bf16[8,96,576]{2,1,0:T(8,128)(2,1)} %bitcast.184, bf16[8,96,192]{2,1,0:T(8,128)(2,1)} %bitcast.191, bf16[8,96,768]{2,1,0:T(8,128)(2,1)} %bitcast.195, bf16[8,96,768]{2,1,0:T(8,128)(2,1)} %bitcast.196), custom_call_target="tpu_custom_call" | custom-call | tf_op jit(solution)/shard_map/pallas_call | solution.py:288
  343.4 1.6 copy.143
  345.1 1.8 copy.140
  346.9 1.8 copy.142
  348.7 1.3 fusion.66
  351.8 1.6 fusion.56
  356.8 3.1 copy.130
  359.8 2.8 fusion.25
  362.7 1.9 copy.151
  364.6 2.8 reshape.251
  368.5 38.7 %psum.22 = f32[2688]{0:T(1024)S(1)} all-reduce(f32[2688]{0:T(1024)S(1)} %concatenate.3), channel_id=1, replica_groups=mesh['dp'=8,'tensor'=4] {'dp'}, use_global_device_ids=true, to_apply=%region_24.25 | all-reduce | flops 2688 | bytes 21504 | tf_op jit(solution)/shard_map/psum | solution.py:516
  409.9 30.5 %all-gather.1 = f32[8,2,1152]{2,1,0:T(2,128)S(1)} all-gather(f32[1,2,1152]{2,1,0:T(2,128)S(1)} %reshape.242), channel_id=1, replica_groups=mesh['dp'=8,'tensor'=4] {'dp'}, dimensions={0}, use_global_device_ids=true | all-gather | bytes 82944 | tf_op jit(solution)/shard_map/all_gather | solution.py:482
  441.3 3.3 all-to-all-start
  447.4 3.6 all-to-all-done
  451.1 10.1 %all-reduce.1 = (f32[2,768]{1,0:T(2,128)S(1)}, f32[1536]{0:T(1024)S(1)}) all-reduce(f32[2,768]{1,0:T(2,128)S(1)} %reshape.229, f32[1536]{0:T(1024)S(1)} %slice.83), channel_id=1, replica_groups=mesh['dp'=8,'tensor'=4] {'tensor'}, use_global_device_ids=true, to_apply=%region_17.18 | all-reduce | flops 3072 | bytes 24576 | tf_op jit(solution)/shard_map/psum | solution.py:494
  (220 shorter events, 43.6 us)
Async XLA Ops:
  7.2 37.1 %copy-start.51 = (f32[2,192]{1,0:T(2,128)S(1)}, f32[2,192]{1,0:T(2,128)}, u32[]{:S(2)}) copy-start(f32[2,192]{1,0:T(2,128)} %param.18) | copy-start | bytes 4612
  7.2 37.3 %copy-start.30 = (bf16[192,96]{1,0:T(8,128)(2,1)S(1)}, bf16[192,96]{1,0:T(8,128)(2,1)}, u32[]{:S(2)}) copy-start(bf16[192,96]{1,0:T(8,128)(2,1)} %param.19) | copy-start | bytes 110596
  7.2 38.0 %copy-start.28 = (bf16[96,3,192]{2,0,1:T(8,128)(2,1)S(1)}, bf16[96,3,192]{2,0,1:T(8,128)(2,1)}, u32[]{:S(2)}) copy-start(bf16[96,3,192]{2,0,1:T(8,128)(2,1)} %param.17) | copy-start | bytes 331780
  7.2 105.3 %all-reduce.4.cloned.1.call-start = ((), (), s32[]{:S(2)}) async-start(), calls=%async_computation.11 | async-start | bytes 147456
  39.9 4.6 copy-start.29
  41.1 44.5 %copy-start.11 = (bf16[96,6,192]{0,2,1:T(8,128)(2,1)}, bf16[96,6,192]{0,2,1:T(8,128)(2,1)S(1)}, u32[]{:S(2)}) copy-start(bf16[96,6,192]{0,2,1:T(8,128)(2,1)S(1)} %copy.109) | copy-start | bytes 663556
  42.0 120.3 %reduce-scatter.8.cloned.1.call-start = ((), (), s32[]{:S(2)}) async-start(), calls=%async_computation.6 | async-start | bytes 983040 | tf_op jit(solution)/shard_map/reduce_scatter | solution.py:60
  43.1 80.5 %copy-start.33 = (f32[128]{0:T(128)}, f32[128]{0:T(128)S(1)}, u32[]{:S(2)}) copy-start(f32[128]{0:T(128)S(1)} %broadcast_multiply_fusion.5) | copy-start | bytes 1540
  43.1 42.5 %copy-start.59 = (u32[32]{0:T(128)S(1)}, u32[32]{0:T(128)}, u32[]{:S(2)}) copy-start(u32[32]{0:T(128)} %constant.67) | copy-start | bytes 388
  44.3 69.1 %copy-start.44 = (f32[6,192]{1,0:T(8,128)S(1)}, f32[6,192]{1,0:T(8,128)}, u32[]{:S(2)}) copy-start(f32[6,192]{1,0:T(8,128)} %param.16) | copy-start | bytes 13828
  44.3 79.3 %copy-start.40 = (f32[128]{0:T(128)}, f32[128]{0:T(128)S(1)}, u32[]{:S(2)}) copy-start(f32[128]{0:T(128)S(1)} %add_rsqrt_fusion.1) | copy-start | bytes 1540
  44.5 91.5 %copy-start.42 = (f32[3,64]{1,0:T(4,128)}, f32[3,64]{1,0:T(4,128)S(1)}, u32[]{:S(2)}) copy-start(f32[3,64]{1,0:T(4,128)S(1)} %add.182) | copy-start | bytes 2308
  86.9 36.8 %copy-start.52 = (s32[128]{0:T(128)}, s32[128]{0:T(128)S(1)}, u32[]{:S(2)}) copy-start(s32[128]{0:T(128)S(1)} %and_select_fusion) | copy-start | bytes 1540
  137.6 24.7 %copy-start.31 = (f32[768]{0:T(1024)S(1)}, f32[768]{0:T(1024)}, u32[]{:S(2)}) copy-start(f32[768]{0:T(1024)} %param.20) | copy-start | bytes 9220
  138.5 25.0 %copy-start.9 = (bf16[128,768]{1,0:T(8,128)(2,1)S(1)}, bf16[128,768]{1,0:T(8,128)(2,1)}, u32[]{:S(2)}) copy-start(bf16[128,768]{1,0:T(8,128)(2,1)} %param.25) | copy-start | bytes 589828
  139.9 71.0 %reduce-scatter.12.cloned.1.call-start = ((), (), s32[]{:S(2)}) async-start(), calls=%async_computation.8 | async-start | bytes 983040 | tf_op jit(solution)/shard_map/reduce_scatter | solution.py:60
  163.4 8.6 %copy-start.36 = (f32[128]{0:T(128)}, f32[128]{0:T(128)S(1)}, u32[]{:S(2)}) copy-start(f32[128]{0:T(128)S(1)} %broadcast_multiply_fusion.4) | copy-start | bytes 1540
  163.6 8.4 %copy-start.45 = (f32[128]{0:T(128)}, f32[128]{0:T(128)S(1)}, u32[]{:S(2)}) copy-start(f32[128]{0:T(128)S(1)} %add_rsqrt_fusion) | copy-start | bytes 1540
  163.6 17.1 %copy-start.57 = (bf16[8,96,768]{2,1,0:T(8,128)(2,1)S(1)}, bf16[8,96,768]{2,1,0:T(8,128)(2,1)}, u32[]{:S(2)}) copy-start(bf16[8,96,768]{2,1,0:T(8,128)(2,1)} %get-tuple-element.23) | copy-start | bytes 3538948
  163.6 17.1 %copy-start.58 = (f32[768]{0:T(1024)S(1)}, f32[768]{0:T(1024)}, u32[]{:S(2)}) copy-start(f32[768]{0:T(1024)} %param.22) | copy-start | bytes 9220
  172.0 9.7 %copy-start.21 = (bf16[512,768]{1,0:T(8,128)(2,1)}, bf16[512,768]{1,0:T(8,128)(2,1)S(1)}, u32[]{:S(2)}) copy-start(bf16[512,768]{1,0:T(8,128)(2,1)S(1)} %all_gather.25) | copy-start | bytes 2359300
  186.9 23.9 %copy-start.37 = (f32[128]{0:T(128)S(1)}, f32[128]{0:T(128)}, u32[]{:S(2)}) copy-start(f32[128]{0:T(128)} %copy-done.36) | copy-start | bytes 1540
  186.9 23.9 %copy-start.46 = (f32[128]{0:T(128)S(1)}, f32[128]{0:T(128)}, u32[]{:S(2)}) copy-start(f32[128]{0:T(128)} %copy-done.45) | copy-start | bytes 1540
  186.9 49.5 %reduce-scatter.10.cloned.1.call-start = ((), (), s32[]{:S(2)}) async-start(), calls=%async_computation.7 | async-start | bytes 983040 | tf_op jit(solution)/shard_map/reduce_scatter | solution.py:60
  190.7 158.0 %reduce-scatter.14.cloned.1.call-start = ((), (), s32[]{:S(2)}) async-start(), calls=%async_computation.9 | async-start | bytes 983040 | tf_op jit(solution)/shard_map/reduce_scatter | solution.py:60
  236.4 10.9 %copy-start.17 = (bf16[8,96,192]{2,1,0:T(8,128)(2,1)S(1)}, bf16[8,96,192]{2,1,0:T(8,128)(2,1)}, u32[]{:S(2)}) copy-start(bf16[8,96,192]{2,1,0:T(8,128)(2,1)} %get-tuple-element.22) | copy-start | bytes 884740
  254.1 4.4 copy-start.19
  277.6 130.8 %reduce-scatter.16.cloned.1.call-start = ((), (), s32[]{:S(2)}) async-start(), calls=%async_computation.10 | async-start | bytes 245760
  292.3 56.4 %copy-start.34 = (f32[128]{0:T(128)S(1)}, f32[128]{0:T(128)}, u32[]{:S(2)}) copy-start(f32[128]{0:T(128)} %copy-done.33) | copy-start | bytes 1540
  348.7 4.8 %copy-start.24 = (bf16[128,768]{1,0:T(8,128)(2,1)S(1)}, bf16[128,768]{1,0:T(8,128)(2,1)}, u32[]{:S(2)}) copy-start(bf16[128,768]{1,0:T(8,128)(2,1)} %reduce-scatter.8.cloned.1.call-done) | copy-start | bytes 589828
  350.0 4.3 copy-start.8
  350.0 5.1 %copy-start.38 = (f32[128]{0:T(128)S(1)}, f32[128]{0:T(128)}, u32[]{:S(2)}) copy-start(f32[128]{0:T(128)} %copy-done.36) | copy-start | bytes 1540
  350.0 5.0 %copy-start.47 = (f32[128]{0:T(128)S(1)}, f32[128]{0:T(128)}, u32[]{:S(2)}) copy-start(f32[128]{0:T(128)} %copy-done.45) | copy-start | bytes 1540
  351.8 4.1 copy-start.10
  351.8 4.1 copy-start.20
  351.8 4.1 copy-start.32
  362.7 4.8 %copy-start.35 = (f32[128]{0:T(128)S(1)}, f32[128]{0:T(128)}, u32[]{:S(2)}) copy-start(f32[128]{0:T(128)} %copy-done.33) | copy-start | bytes 1540
  362.7 4.8 %copy-start.41 = (f32[128]{0:T(128)S(1)}, f32[128]{0:T(128)}, u32[]{:S(2)}) copy-start(f32[128]{0:T(128)} %copy-done.40) | copy-start | bytes 1540
  362.7 4.8 %copy-start.54 = (f32[128]{0:T(128)S(1)}, f32[128]{0:T(128)}, u32[]{:S(2)}) copy-start(f32[128]{0:T(128)} %broadcast_multiply_fusion) | copy-start | bytes 1540
  362.7 4.8 %copy-start.55 = (f32[128]{0:T(128)S(1)}, f32[128]{0:T(128)}, u32[]{:S(2)}) copy-start(f32[128]{0:T(128)} %broadcast_multiply_fusion.1) | copy-start | bytes 1540
  364.6 3.8 copy-start.48
  364.6 3.8 copy-start.49
  364.6 3.8 copy-start.50
  367.4 73.0 %copy-start.12 = (bf16[96,6,192]{0,2,1:T(8,128)(2,1)S(1)}, bf16[96,6,192]{0,2,1:T(8,128)(2,1)}, u32[]{:S(2)}) copy-start(bf16[96,6,192]{0,2,1:T(8,128)(2,1)} %copy-done.11) | copy-start | bytes 663556
  409.5 51.8 %copy-start.39 = (bf16[2,768]{1,0:T(2,128)(2,1)S(1)}, bf16[2,768]{1,0:T(2,128)(2,1)}, u32[]{:S(2)}) copy-start(bf16[2,768]{1,0:T(2,128)(2,1)} %param.14) | copy-start | bytes 9220
  409.5 53.0 %copy-start.27 = (f32[96,768]{1,0:T(8,128)S(1)}, f32[96,768]{1,0:T(8,128)}, u32[]{:S(2)}) copy-start(f32[96,768]{1,0:T(8,128)} %get-tuple-element.142) | copy-start | bytes 884740
  440.4 22.8 %copy-start.26 = (f32[96,768]{1,0:T(8,128)S(1)}, f32[96,768]{1,0:T(8,128)}, u32[]{:S(2)}) copy-start(f32[96,768]{1,0:T(8,128)} %get-tuple-element.28) | copy-start | bytes 884740
  441.3 9.8 %all-to-all-start = ((f32[8,2,96]{2,1,0:T(2,128)}), f32[8,2,96]{2,1,0:T(2,128)S(1)}, u32[]{:S(2)}, u32[]{:S(2)}) async-start(f32[8,2,96]{2,1,0:T(2,128)} %copy.134), calls=%async_computation.4 | async-start | bytes 16384 | tf_op jit(solution)/shard_map/all_to_all | solution.py:491
  (22 other events, 41.1 us)
Sparse Core Ops, SparseCore 0:
  42.1 70.2 all-reduce.3
  140.0 22.2 reduce-scatter.7
  187.0 23.7 reduce-scatter.11
  213.2 23.1 reduce-scatter.9
  277.7 23.7 reduce-scatter.13
  367.6 24.6 reduce-scatter.15

commit v3 on v2

--- a/solution.py
+++ b/solution.py
@@ -56,10 +56,10 @@
     return lax.all_gather(values, "tensor", axis=0, tiled=True)
 
 
-def sum_rows(values):
-    return lax.psum_scatter(
-        values.astype(jnp.bfloat16), "tensor", scatter_dimension=0, tiled=True
-    ).astype(jnp.float32)
+def sum_rows(values, number):
+    size = lax.axis_size("tensor")
+    blocks = values.astype(jnp.bfloat16).reshape(size, -1, values.shape[1])
+    return jnp.sum(exchange("tensor", True, number, blocks)[0].astype(jnp.float32), axis=0)
 
 
 MESH = pl.DeviceIdType.MESH
@@ -299,6 +299,76 @@
         ],
         compiler_params=pltpu.CompilerParams(collective_id=1, has_side_effects=True),
     )(*parts)
+
+
+def exchange_kernel(axis, size, spread, count, *refs):
+    ins, outs = refs[:count], refs[count : 2 * count]
+    own_sem, send_sem, recv_sem = refs[2 * count :]
+    me = lax.axis_index(axis)
+    barrier = pltpu.get_barrier_semaphore()
+
+    def peer(shift):
+        other = lax.rem(me + shift, size)
+        places = {name: lax.axis_index(name) for name in ("dp", "tensor")}
+        places[axis] = other
+        return other, (places["dp"], places["tensor"])
+
+    def send(item, shift):
+        other, target = peer(shift)
+        return pltpu.make_async_remote_copy(
+            src_ref=ins[item].at[other] if spread else ins[item],
+            dst_ref=outs[item].at[me],
+            send_sem=send_sem.at[item, shift - 1],
+            recv_sem=recv_sem.at[item, shift - 1],
+            device_id=target,
+            device_id_type=MESH,
+        )
+
+    def arrive(item, shift):
+        other, target = peer(size - shift)
+        return pltpu.make_async_remote_copy(
+            src_ref=outs[item].at[other],
+            dst_ref=outs[item].at[other],
+            send_sem=send_sem.at[item, shift - 1],
+            recv_sem=recv_sem.at[item, shift - 1],
+            device_id=target,
+            device_id_type=MESH,
+        )
+
+    def own(item):
+        source = ins[item].at[me] if spread else ins[item]
+        return pltpu.make_async_copy(source, outs[item].at[me], own_sem.at[item])
+
+    for shift in range(1, size):
+        pl.semaphore_signal(barrier, inc=1, device_id=peer(shift)[1], device_id_type=MESH)
+    for item in range(count):
+        own(item).start()
+    pl.semaphore_wait(barrier, size - 1)
+    for item in range(count):
+        for shift in range(1, size):
+            send(item, shift).start()
+    for item in range(count):
+        own(item).wait()
+        for shift in range(1, size):
+            arrive(item, shift).wait_recv()
+            send(item, shift).wait_send()
+
+
+def exchange(axis, spread, number, *values):
+    size, count = lax.axis_size(axis), len(values)
+    shapes = [v.shape if spread else (size,) + v.shape for v in values]
+    return pl.pallas_call(
+        functools.partial(exchange_kernel, axis, size, spread, count),
+        out_shape=[jax.ShapeDtypeStruct(s, v.dtype) for s, v in zip(shapes, values)],
+        in_specs=[VMEM] * count,
+        out_specs=[VMEM] * count,
+        scratch_shapes=[
+            pltpu.SemaphoreType.DMA((count,)),
+            pltpu.SemaphoreType.DMA((count, size - 1)),
+            pltpu.SemaphoreType.DMA((count, size - 1)),
+        ],
+        compiler_params=pltpu.CompilerParams(collective_id=number, has_side_effects=True),
+    )(*values)
 
 
 def attend(query_rows, key_rows, value_rows):
@@ -374,18 +444,23 @@
         (entry_flat, output_weight.T, expand_weight, reduce_weight.T)
     )
     condition_float = condition.astype(jnp.float32)
-    condition_all = lax.all_gather(condition, "dp", axis=0, tiled=True)
+    condition_all = exchange("dp", False, 2, condition)[0].reshape(-1, features)
     soft_all = jax.nn.silu(condition_all.astype(jnp.float32)).astype(jnp.bfloat16)
     soft_mine = lax.dynamic_slice_in_dim(soft_all, dp_index * shard_rows, shard_rows, 1)
     adaptive_flat = adaptive_weight.reshape(shard_rows, 6 * local_width)
     modulation_partial = jnp.dot(soft_mine, adaptive_flat, preferred_element_type=jnp.float32)
     modulation_local = (
-        lax.psum_scatter(modulation_partial, "dp", scatter_dimension=0, tiled=True).reshape(
-            seq_count, 6, local_width
-        )
+        jnp.sum(
+            exchange("dp", True, 3, modulation_partial.reshape(dp_count, seq_count, -1))[0], axis=0
+        ).reshape(seq_count, 6, local_width)
         + adaptive_bias[None]
     )
-    modulation = lax.all_gather(modulation_local, "tensor", axis=2, tiled=True)
+    modulation = (
+        exchange("tensor", False, 4, modulation_local.reshape(seq_count, -1))[0]
+        .reshape(tensor_count, seq_count, 6, local_width)
+        .transpose(1, 2, 0, 3)
+        .reshape(seq_count, 6, features)
+    )
     seq_of_row = (tensor_index * row_count + jnp.arange(row_count, dtype=jnp.int32)) // LEN
     selector = (seq_of_row[:, None] == jnp.arange(seq_count, dtype=jnp.int32)[None, :]).astype(
         jnp.float32
@@ -411,7 +486,7 @@
     attended, log_total = attend(query_rows, key_rows, value_rows)
     attended = attended.reshape(group_rows, local_width)
     attention_branch = (
-        sum_rows(contract_last(attended, output_full)) + output_bias
+        sum_rows(contract_last(attended, output_full), 9) + output_bias
     )
     middle = inputs + gate_one * attention_branch
     normed_two, inverse_two = norm_rows(middle)
@@ -421,7 +496,7 @@
     hidden_value, hidden_slope = gelu_pair(hidden_pre)
     hidden_rows = hidden_value.astype(jnp.bfloat16)
     feed_branch = (
-        sum_rows(contract_last(hidden_rows, reduce_full))
+        sum_rows(contract_last(hidden_rows, reduce_full), 10)
         + reduce_bias
     )
     block_output = (middle + gate_two * feed_branch).astype(jnp.bfloat16)
@@ -432,7 +507,7 @@
     hidden_grad = jnp.dot(feed_gathered, reduce_full, preferred_element_type=jnp.float32) * hidden_slope
     hidden_round = hidden_grad.astype(jnp.bfloat16)
     expand_total = contract_first(feed_input, hidden_round)
-    feed_input_grad = sum_rows(contract_last(hidden_round, expand_full))
+    feed_input_grad = sum_rows(contract_last(hidden_round, expand_full), 11)
     middle_grad = upstream + norm_back(feed_input_grad * (1.0 + scale_two), normed_two, inverse_two)
     attention_grad = middle_grad * gate_one
     attention_gathered = gather_rows(attention_grad.astype(jnp.bfloat16))
@@ -454,7 +529,7 @@
         .reshape(group_rows, 3 * local_width)
     )
     entry_total = contract_first(attention_input, entry_round)
-    input_grad = sum_rows(contract_last(entry_round, entry_full))
+    input_grad = sum_rows(contract_last(entry_round, entry_full), 12)
     tokens_gradient = middle_grad + norm_back(
         input_grad * (1.0 + scale_one), normed_one, inverse_one
     )
@@ -476,34 +551,15 @@
         precision=HIGHEST_PRECISION,
         preferred_element_type=jnp.float32,
     ).reshape(seq_count, 6, features)
-    modulation_grad = lax.psum_scatter(
-        per_sequence.astype(jnp.bfloat16), "tensor", scatter_dimension=2, tiled=True
-    ).astype(jnp.float32)
-    modulation_all = lax.all_gather(
-        modulation_grad.reshape(seq_count, 6 * local_width), "dp", axis=0, tiled=True
-    )
-    bias_adaptive = jnp.sum(modulation_all, axis=0).reshape(6, local_width)
-    modulation_round = modulation_all.astype(jnp.bfloat16)
-    adaptive_gradient = contract_first(soft_mine, modulation_round).reshape(
-        shard_rows, 6, local_width
-    )
-    condition_partial = contract_last(modulation_round, adaptive_flat)
-    condition_moved = lax.all_to_all(
-        condition_partial.reshape(dp_count, seq_count, shard_rows), "dp", 0, 0
-    )
-    condition_sum = lax.psum(
-        condition_moved.transpose(1, 0, 2).reshape(seq_count, features), "tensor"
-    )
-    sigmoid_value = jax.nn.sigmoid(condition_float)
-    condition_gradient = (
-        condition_sum * sigmoid_value * (1.0 + condition_float * (1.0 - sigmoid_value))
-    )
-    entry_gradient, output_gradient, expand_gradient, reduce_gradient = scatter_gradients(
-        (entry_total, output_total, expand_total, reduce_total)
-    )
-    entry_gradient = entry_gradient.reshape(shard_rows, 3, local_width)
-    output_gradient = output_gradient.T
-    reduce_gradient = reduce_gradient.T
+    sequence_parts = (
+        per_sequence.astype(jnp.bfloat16)
+        .reshape(seq_count, 6, tensor_count, local_width)
+        .transpose(2, 0, 1, 3)
+        .reshape(tensor_count, seq_count, 6 * local_width)
+    )
+    modulation_grad = jnp.sum(
+        exchange("tensor", True, 5, sequence_parts)[0].astype(jnp.float32), axis=0
+    )
     own_sums = jnp.concatenate(
         [
             jnp.sum(query_grad, axis=0),
@@ -513,11 +569,40 @@
             jnp.sum(feed_grad, axis=0),
         ]
     )
-    dp_sums = lax.psum(own_sums, "dp")
+    modulation_all, sums_all = exchange("dp", False, 6, modulation_grad, own_sums[None])
+    modulation_all = modulation_all.reshape(dp_count * seq_count, 6 * local_width)
+    dp_sums = jnp.sum(sums_all, axis=(0, 1))
+    bias_adaptive = jnp.sum(modulation_all, axis=0).reshape(6, local_width)
+    modulation_round = modulation_all.astype(jnp.bfloat16)
+    adaptive_gradient = contract_first(soft_mine, modulation_round).reshape(
+        shard_rows, 6, local_width
+    )
+    condition_partial = contract_last(modulation_round, adaptive_flat)
+    condition_moved = exchange(
+        "dp", True, 7, condition_partial.reshape(dp_count, seq_count, shard_rows)
+    )[0]
     own_width = 2 * local_width + local_hidden
+    condition_parts, row_parts = exchange(
+        "tensor",
+        False,
+        8,
+        condition_moved.transpose(1, 0, 2).reshape(seq_count, features),
+        dp_sums[None, own_width:],
+    )
+    condition_sum = jnp.sum(condition_parts, axis=0)
+    row_sums = jnp.sum(row_parts, axis=(0, 1))
+    sigmoid_value = jax.nn.sigmoid(condition_float)
+    condition_gradient = (
+        condition_sum * sigmoid_value * (1.0 + condition_float * (1.0 - sigmoid_value))
+    )
+    entry_gradient, output_gradient, expand_gradient, reduce_gradient = scatter_gradients(
+        (entry_total, output_total, expand_total, reduce_total)
+    )
+    entry_gradient = entry_gradient.reshape(shard_rows, 3, local_width)
+    output_gradient = output_gradient.T
+    reduce_gradient = reduce_gradient.T
     bias_entry = dp_sums[: 2 * local_width].reshape(2, local_width)
     bias_expand = dp_sums[2 * local_width : own_width]
-    row_sums = lax.psum(dp_sums[own_width:], "tensor")
     output_sums = row_sums[:features]
     reduce_sums = row_sums[features:]
     return (

time: 472 us -> 360 us (0.76)
  blocking collectives: 154 us -> 37 us
  Pallas kernels: 88.9 us -> 202 us
  waiting for transfers between devices: 95.5 us -> 0 us
  between operations: 15.5 us -> 1.42 us
  other arithmetic: 18.4 us -> 27.8 us
    pallas_call x0 -> x11, Pallas kernels: none -> 106 us  [exchange(): pl.pallas_call(functools.partial(exchange_kernel, axis, size, spread, cou...]
    all_gather x3 -> x0, blocking collectives: 71.7 us -> none  [the longest x1 32.6 us: body(): condition_all = lax.all_gather(condition, 'dp', axis=0, tiled=True)]
    reduce_scatter x4 -> x0, waiting for transfers between devices: 66.2 us -> none  [sum_rows(): lax.psum_scatter(values.astype(jnp.bfloat16), 'tensor', scatter_dimension...]
    psum x2 -> x0, blocking collectives: 48.8 us -> none  [the longest x1 38.7 us: body(): dp_sums = lax.psum(own_sums, 'dp')]
    unnamed x8 -> x0, waiting for transfers between devices: 25.7 us -> none
    reduce_sum x0 -> x9, other arithmetic: none -> 10.1 us  [the longest x4 5.31 us: sum_rows(): jnp.sum(exchange('tensor', True, number, blocks)[0].astype(jnp.float32),...]
    unnamed x142 -> x110, local copies, waits for them, and re-layouts: 20.5 us -> 11.6 us
    pallas_call x1, Pallas kernels: 37.9 us -> 44.9 us  [gather_weights(): pl.pallas_call(functools.partial(gather_kernel, length, count), out_shape...]
  transfers between devices with their start and end apart: 7 -> 0, of which waited for: 5 -> 0; matrix products, arithmetic and copies ran while one was open for 8% -> 0% of each run, Pallas kernels for 19% -> 0%
where the time goes in v3:
time: 360 us; the launch traced here: 357 us
  Pallas kernels  202 us (56%)
  local copies, waits for them, and re-layouts  49.7 us (14%)
  matrix products  39.3 us (11%)
  blocking collectives  37 us (10%)
  other arithmetic  27.8 us (8%)
    pallas_call x11, Pallas kernels, exchange(): pl.pallas_call(functools.partial(exchange_kernel, axis, size, spread, cou...  106 us
    pallas_call x1, Pallas kernels, scatter_gradients(): pl.pallas_call(functools.partial(scatter_kernel, length, count), out_shap...  51.1 us
    pallas_call x1, Pallas kernels, gather_weights(): pl.pallas_call(functools.partial(gather_kernel, length, count), out_shape...  44.9 us
    all_gather x4, blocking collectives, gather_rows(): return lax.all_gather(values, 'tensor', axis=0, tiled=True)  37 us
    unnamed x110, local copies, waits for them, and re-layouts  11.6 us
    dot_general x5, matrix products, contract_last(): lax.dot_general(left, right, (((1,), (1,)), ((), ())), preferred_element_...  8.09 us
    dot_general x5, matrix products, contract_first(): lax.dot_general(left, right, (((0,), (0,)), ((), ())), preferred_element_...  7.47 us

profile of v3, /device:TPU:0, one launch (start us, length us, event | category | flops | bytes accessed | tf_op | source)
XLA Modules:
  0.0 357.4 jit_solution(12116197816470166304)
XLA Ops:
  4.6 9.7 %shard_map.228 = bf16[8,2,768]{2,1,0:T(2,128)(2,1)} custom-call(bf16[2,768]{1,0:T(2,128)(2,1)} %refs_0_.1), custom_call_target="tpu_custom_call" | custom-call | tf_op jit(solution)/shard_map/pallas_call | solution.py:360
  15.1 1.5 copy.91
  20.6 8.3 %shard_map.229 = f32[8,2,1152]{2,1,0:T(2,128)} custom-call(f32[8,2,1152]{2,1,0:T(2,128)} %copy.87.refs_0_), custom_call_target="tpu_custom_call" | custom-call | tf_op jit(solution)/shard_map/pallas_call | solution.py:360
  30.4 5.0 %shard_map.230 = f32[4,2,1152]{2,1,0:T(2,128)} custom-call(f32[2,1152]{1,0:T(2,128)} %broadcast_add_fusion.refs_0_), custom_call_target="tpu_custom_call" | custom-call | tf_op jit(solution)/shard_map/pallas_call | solution.py:360
  37.9 9.1 %all_gather.12 = bf16[512,768]{1,0:T(8,128)(2,1)} all-gather(bf16[128,768]{1,0:T(8,128)(2,1)S(1)} %fusion.44), channel_id=1, replica_groups=mesh['dp'=8,'tensor'=4] {'tensor'}, dimensions={0}, use_global_device_ids=true | all-gather | bytes 983040 | tf_op jit(solution)/shard_map/all_gather | solution.py:56
  47.0 44.9 %shard_map.231 = (bf16[8,96,576]{2,1,0:T(8,128)(2,1)}, bf16[8,96,192]{2,1,0:T(8,128)(2,1)}, bf16[8,96,768]{2,1,0:T(8,128)(2,1)}, bf16[8,96,768]{2,1,0:T(8,128)(2,1)}) custom-call(bf16[96,576]{1,0:T(8,128)(2,1)} %copy.92.refs_0_, bf16[96,192]{1,0:T(8,128)(2,1)} %bitcast.207, bf16[96,768]{1,0:T(8,128)(2,1)} %refs_2_.1, bf16[96,768]{1,0:T(8,128)(2,1)} %bitcast.208), custom_call_target="tpu_custom_call" | custom-call | tf_op jit(solution)/shard_map/pallas_call | solution.py:176
  91.9 2.2 copy.93
  94.1 2.1 fusion.29
  100.6 1.3 convolution_convert_fusion.6
  101.9 12.4 %shard_map.232 = bf16[4,128,768]{2,1,0:T(8,128)(2,1)} custom-call(bf16[4,128,768]{2,1,0:T(8,128)(2,1)} %bitcast.185), custom_call_target="tpu_custom_call" | custom-call | tf_op jit(solution)/shard_map/pallas_call | solution.py:360
  114.4 1.3 convert_reduce_fusion.3
  117.0 9.4 %all_gather.14 = bf16[512,768]{1,0:T(8,128)(2,1)S(1)} all-gather(bf16[128,768]{1,0:T(8,128)(2,1)S(1)} %get-tuple-element.91), channel_id=1, replica_groups=mesh['dp'=8,'tensor'=4] {'tensor'}, dimensions={0}, use_global_device_ids=true | all-gather | bytes 983040 | tf_op jit(solution)/shard_map/all_gather | solution.py:56
  126.4 8.9 %all_gather.13 = bf16[512,768]{1,0:T(8,128)(2,1)S(1)} all-gather(bf16[128,768]{1,0:T(8,128)(2,1)S(1)} %get-tuple-element.92), channel_id=1, replica_groups=mesh['dp'=8,'tensor'=4] {'tensor'}, dimensions={0}, use_global_device_ids=true | all-gather | bytes 983040 | tf_op jit(solution)/shard_map/all_gather | solution.py:56
  137.5 2.0 convolution_convert_fusion.4
  139.5 2.0 fusion.112
  141.5 2.0 convolution_convert_fusion
  143.5 1.7 convolution_convert_fusion.3
  145.1 11.7 %shard_map.234 = bf16[4,128,768]{2,1,0:T(8,128)(2,1)} custom-call(bf16[4,128,768]{2,1,0:T(8,128)(2,1)} %bitcast.200), custom_call_target="tpu_custom_call" | custom-call | tf_op jit(solution)/shard_map/pallas_call | solution.py:360
  158.1 12.9 %shard_map.233 = bf16[4,128,768]{2,1,0:T(8,128)(2,1)} custom-call(bf16[4,128,768]{2,1,0:T(8,128)(2,1)} %bitcast.198), custom_call_target="tpu_custom_call" | custom-call | tf_op jit(solution)/shard_map/pallas_call | solution.py:360
  171.0 1.4 convert_reduce_fusion.2
  173.5 1.8 convolution_convert_fusion.1
  176.4 9.6 %all_gather.15 = bf16[512,768]{1,0:T(8,128)(2,1)S(1)} all-gather(bf16[128,768]{1,0:T(8,128)(2,1)S(1)} %get-tuple-element.86), channel_id=1, replica_groups=mesh['dp'=8,'tensor'=4] {'tensor'}, dimensions={0}, use_global_device_ids=true | all-gather | bytes 983040 | tf_op jit(solution)/shard_map/all_gather | solution.py:56
  188.1 1.7 reshape.246
  189.8 1.9 copy.116
  191.7 3.1 fusion.111
  194.8 1.3 reduce_sum.248
  196.1 1.8 copy.107
  197.9 1.7 stack_reshape.11
  199.7 2.6 fusion.70
  202.2 4.4 %fusion.21 = bf16[2,256,3,64]{1,3,2,0:T(8,128)(2,1)} fusion(f32[2,3,256,256]{2,3,1,0:T(8,128)} %fusion.70, f32[2,3,256,256]{2,3,1,0:T(8,128)} %copy-done, f32[2,3,256]{2,1,0:T(4,128)S(1)} %log_add_fusion, f32[2,256,3,64]{1,0,3,2:T(2,128)} %copy-done.16, f32[3,64]{1,0:T(4,128)} %copy-done.36), kind=kOutput, calls=%fused_computation.34 | convolution fusion | flops 53282560 | bytes 3742464 | tf_op jit(solution)/shard_map/bhlm,blhe->bmhe/dot_general | solution.py:408
  206.7 4.3 %fusion.108 = (f32[3,64]{1,0:T(4,128)S(1)}, bf16[2,256,3,64]{1,3,2,0:T(8,128)(2,1)}) fusion(f32[2,3,256,256]{2,3,1,0:T(8,128)} %fusion.70, f32[2,3,256,256]{2,3,1,0:T(8,128)} %copy-done, f32[2,3,256]{2,1,0:T(4,128)S(1)} %log_add_fusion, bf16[2,256,3,64]{1,0,3,2:T(2,128)(2,1)S(1)} %copy-done.20), kind=kOutput, calls=%fused_computation.158 | convolution fusion | flops 53282368 | bytes 3545856 | tf_op jit(solution)/shard_map/bhlm,bmhe->blhe/dot_general | solution.py:405
  211.6 1.8 copy.104
  214.5 1.8 copy.102
  216.3 1.7 stack_reshape.9
  219.0 3.0 convolution_convert_fusion.5
  222.0 1.6 convolution_convert_fusion.2
  223.6 12.4 %shard_map.235 = bf16[4,128,768]{2,1,0:T(8,128)(2,1)} custom-call(bf16[4,128,768]{2,1,0:T(8,128)(2,1)} %bitcast.199), custom_call_target="tpu_custom_call" | custom-call | tf_op jit(solution)/shard_map/pallas_call | solution.py:360
  237.3 1.9 fusion.65
  242.0 2.0 fusion.48
  244.0 2.2 copy.115
  246.3 51.1 %shard_map.240 = (f32[96,576]{1,0:T(8,128)}, f32[96,192]{1,0:T(8,128)}, f32[96,768]{1,0:T(8,128)}, f32[96,768]{1,0:T(8,128)}) custom-call(bf16[8,96,576]{2,1,0:T(8,128)(2,1)} %bitcast.183, bf16[8,96,192]{2,1,0:T(8,128)(2,1)} %bitcast.190, bf16[8,96,768]{2,1,0:T(8,128)(2,1)} %bitcast.194, bf16[8,96,768]{2,1,0:T(8,128)(2,1)} %bitcast.193), custom_call_target="tpu_custom_call" | custom-call | tf_op jit(solution)/shard_map/pallas_call | solution.py:288
  297.5 1.7 copy.119
  306.2 2.0 copy.108
  310.3 5.0 %shard_map.236 = bf16[4,2,1152]{2,1,0:T(2,128)(2,1)} custom-call(bf16[4,2,1152]{2,1,0:T(2,128)(2,1)} %reshape.250.refs_0_), custom_call_target="tpu_custom_call" | custom-call | tf_op jit(solution)/shard_map/pallas_call | solution.py:360
  315.3 1.3 convert_reduce_fusion.5.refs_0_
  316.6 15.6 %shard_map.237 = (f32[8,2,1152]{2,1,0:T(2,128)}, f32[8,1,2688]{2,1,0:T(1,128)}) custom-call(f32[2,1152]{1,0:T(2,128)} %convert_reduce_fusion.5.refs_0_, f32[1,2688]{1,0:T(1,128)} %broadcast_in_dim.4.refs_1_), custom_call_target="tpu_custom_call" | custom-call | tf_op jit(solution)/shard_map/pallas_call | solution.py:360
  334.7 7.8 %shard_map.238 = f32[8,2,96]{2,1,0:T(2,128)} custom-call(f32[8,2,96]{2,1,0:T(2,128)} %copy.112.refs_0_), custom_call_target="tpu_custom_call" | custom-call | tf_op jit(solution)/shard_map/pallas_call | solution.py:360
  346.9 5.2 %shard_map.239 = (f32[4,2,768]{2,1,0:T(2,128)}, f32[4,1,1536]{2,1,0:T(1,128)}) custom-call(f32[2,768]{1,0:T(2,128)} %reshape.251.refs_0_, f32[1,1536]{1,0:T(1,128)} %broadcast_in_dim.5.refs_1_), custom_call_target="tpu_custom_call" | custom-call | tf_op jit(solution)/shard_map/pallas_call | solution.py:360
  (187 shorter events, 53.5 us)
Async XLA Ops:
  0.7 35.9 %copy-start.43 = (s32[128]{0:T(128)}, s32[128]{0:T(128)S(1)}, u32[]{:S(2)}) copy-start(s32[128]{0:T(128)S(1)} %and_select_fusion) | copy-start | bytes 1540
  1.7 36.0 %copy-start.32 = (f32[128]{0:T(128)}, f32[128]{0:T(128)S(1)}, u32[]{:S(2)}) copy-start(f32[128]{0:T(128)S(1)} %broadcast_multiply_fusion.5) | copy-start | bytes 1540
  2.9 34.8 %copy-start.40 = (f32[128]{0:T(128)}, f32[128]{0:T(128)S(1)}, u32[]{:S(2)}) copy-start(f32[128]{0:T(128)S(1)} %add_rsqrt_fusion.1) | copy-start | bytes 1540
  3.8 94.8 %copy-start.36 = (f32[3,64]{1,0:T(4,128)}, f32[3,64]{1,0:T(4,128)S(1)}, u32[]{:S(2)}) copy-start(f32[3,64]{1,0:T(4,128)S(1)} %add.168) | copy-start | bytes 2308
  19.7 16.8 %copy-start.12 = (bf16[96,6,192]{0,2,1:T(8,128)(2,1)}, bf16[96,6,192]{0,2,1:T(8,128)(2,1)S(1)}, u32[]{:S(2)}) copy-start(bf16[96,6,192]{0,2,1:T(8,128)(2,1)S(1)} %copy.84) | copy-start | bytes 663556
  19.9 17.8 %copy-start.1 = (bf16[128,768]{1,0:T(8,128)(2,1)S(1)}, bf16[128,768]{1,0:T(8,128)(2,1)}, u32[]{:S(2)}) copy-start(bf16[128,768]{1,0:T(8,128)(2,1)} %param.13) | copy-start | bytes 589828
  97.1 2.0 copy-start.19
  99.1 1.2 copy-start
  99.4 1.3 copy-start.17
  100.5 1.5 copy-start.14
  114.3 2.4 copy-start.9
  116.6 9.9 %copy-start.29 = (f32[128]{0:T(128)}, f32[128]{0:T(128)S(1)}, u32[]{:S(2)}) copy-start(f32[128]{0:T(128)S(1)} %broadcast_multiply_fusion.4) | copy-start | bytes 1540
  116.8 9.6 %copy-start.37 = (f32[128]{0:T(128)}, f32[128]{0:T(128)S(1)}, u32[]{:S(2)}) copy-start(f32[128]{0:T(128)S(1)} %add_rsqrt_fusion) | copy-start | bytes 1540
  116.8 19.4 %copy-start.45 = (bf16[8,96,768]{2,1,0:T(8,128)(2,1)S(1)}, bf16[8,96,768]{2,1,0:T(8,128)(2,1)}, u32[]{:S(2)}) copy-start(bf16[8,96,768]{2,1,0:T(8,128)(2,1)} %get-tuple-element.27) | copy-start | bytes 3538948
  116.8 19.4 %copy-start.47 = (f32[768]{0:T(1024)S(1)}, f32[768]{0:T(1024)}, u32[]{:S(2)}) copy-start(f32[768]{0:T(1024)} %param.22) | copy-start | bytes 9220
  135.3 0.9 copy-start.22
  136.2 1.3 copy-start.46
  141.5 2.0 copy-start.48
  171.0 2.4 copy-start.23
  171.0 2.4 copy-start.49
  172.5 2.9 copy-start.6
  173.4 1.9 copy-start.10
  173.4 1.9 copy-start.27
  173.5 1.9 copy-start.30
  173.5 1.9 copy-start.38
  175.3 10.6 %copy-start.18 = (bf16[8,96,192]{2,1,0:T(8,128)(2,1)S(1)}, bf16[8,96,192]{2,1,0:T(8,128)(2,1)}, u32[]{:S(2)}) copy-start(bf16[8,96,192]{2,1,0:T(8,128)(2,1)} %get-tuple-element.26) | copy-start | bytes 884740
  176.4 10.7 %copy-start.15 = (bf16[24,8,2,256]{3,1,2,0:T(8,128)(2,1)S(1)}, bf16[24,8,2,256]{3,1,2,0:T(8,128)(2,1)}, u32[]{:S(2)}) copy-start(bf16[24,8,2,256]{3,1,2,0:T(8,128)(2,1)} %copy-done.14) | copy-start | bytes 589828
  202.2 4.4 %copy-start.20 = (bf16[2,256,3,64]{1,0,3,2:T(2,128)(2,1)S(1)}, bf16[2,256,3,64]{1,0,3,2:T(2,128)(2,1)}, u32[]{:S(2)}) copy-start(bf16[2,256,3,64]{1,0,3,2:T(2,128)(2,1)} %copy-done.19) | copy-start | bytes 589828
  206.7 11.3 %copy-start.21 = (bf16[512,1,192]{0,2,1:T(8,128)(2,1)S(1)}, bf16[512,1,192]{0,2,1:T(8,128)(2,1)}, u32[]{:S(2)}) copy-start(bf16[512,1,192]{0,2,1:T(8,128)(2,1)} %stack_reshape.11) | copy-start | bytes 589828
  219.0 3.0 copy-start.8
  223.6 13.7 %copy-start.33 = (f32[128]{0:T(128)S(1)}, f32[128]{0:T(128)}, u32[]{:S(2)}) copy-start(f32[128]{0:T(128)} %copy-done.32) | copy-start | bytes 1540
  223.6 13.7 %copy-start.41 = (f32[128]{0:T(128)S(1)}, f32[128]{0:T(128)}, u32[]{:S(2)}) copy-start(f32[128]{0:T(128)} %copy-done.40) | copy-start | bytes 1540
  297.4 4.5 %copy-start.2 = (bf16[128,768]{1,0:T(8,128)(2,1)S(1)}, bf16[128,768]{1,0:T(8,128)(2,1)}, u32[]{:S(2)}) copy-start(bf16[128,768]{1,0:T(8,128)(2,1)} %param.13) | copy-start | bytes 589828
  297.4 4.5 %copy-start.34 = (f32[128]{0:T(128)S(1)}, f32[128]{0:T(128)}, u32[]{:S(2)}) copy-start(f32[128]{0:T(128)} %copy-done.32) | copy-start | bytes 1540
  297.4 4.5 %copy-start.42 = (f32[128]{0:T(128)S(1)}, f32[128]{0:T(128)}, u32[]{:S(2)}) copy-start(f32[128]{0:T(128)} %copy-done.40) | copy-start | bytes 1540
  297.4 5.4 %copy-start.3 = (f32[128,768]{1,0:T(8,128)S(1)}, f32[128,768]{1,0:T(8,128)}, u32[]{:S(2)}) copy-start(f32[128,768]{1,0:T(8,128)} %get-tuple-element.87) | copy-start | bytes 1179652
  297.4 5.4 %copy-start.5 = (f32[128,768]{1,0:T(8,128)S(1)}, f32[128,768]{1,0:T(8,128)}, u32[]{:S(2)}) copy-start(f32[128,768]{1,0:T(8,128)} %copy-done.4) | copy-start | bytes 1179652
  297.4 5.4 %copy-start.26 = (f32[768]{0:T(1024)S(1)}, f32[768]{0:T(1024)}, u32[]{:S(2)}) copy-start(f32[768]{0:T(1024)} %param.20) | copy-start | bytes 9220
  301.9 2.6 copy-start.31
  301.9 2.6 copy-start.39
  302.8 2.5 copy-start.7
  302.8 2.5 copy-start.11
  302.9 2.5 copy-start.28
  306.2 2.0 copy-start.44
  308.2 25.1 %copy-start.13 = (bf16[96,6,192]{0,2,1:T(8,128)(2,1)S(1)}, bf16[96,6,192]{0,2,1:T(8,128)(2,1)}, u32[]{:S(2)}) copy-start(bf16[96,6,192]{0,2,1:T(8,128)(2,1)} %copy-done.12) | copy-start | bytes 663556
  308.2 45.5 %copy-start.35 = (bf16[2,768]{1,0:T(2,128)(2,1)S(1)}, bf16[2,768]{1,0:T(2,128)(2,1)}, u32[]{:S(2)}) copy-start(bf16[2,768]{1,0:T(2,128)(2,1)} %refs_0_.1) | copy-start | bytes 9220
  308.2 47.7 %copy-start.25 = (f32[96,768]{1,0:T(8,128)S(1)}, f32[96,768]{1,0:T(8,128)}, u32[]{:S(2)}) copy-start(f32[96,768]{1,0:T(8,128)} %get-tuple-element.137) | copy-start | bytes 884740
  309.4 47.3 %copy-start.24 = (f32[96,768]{1,0:T(8,128)S(1)}, f32[96,768]{1,0:T(8,128)}, u32[]{:S(2)}) copy-start(f32[96,768]{1,0:T(8,128)} %get-tuple-element.36) | copy-start | bytes 884740
  (2 other events, 1.6 us)
